TPU v7x, 32 devices: a whole 2x2x4 slice. The times are simulated.
32 devices in a mesh: grp: 2 (over y), blk: 4 (over z), head: 4 (over x, core).
Axes of the slice: x: 2, y: 2, z: 4, core: 2. Of those that a mesh axis runs over, the one named last changes fastest.
Arguments:
- queries: bfloat16 [8, 576, 4096], P('grp', None, ('head', 'blk')), parts along dimension 0, may hold values from -8 to 8
- tree_keys: bfloat16 [8, 32, 576], P('grp'), parts along dimension 0, may hold values from -8 to 8
- parents: int32 [8, 32], P('grp'), parts along dimension 0, may hold values from 0 to 30, as said below
- node_live: int32 [8, 32], P('grp'), parts along dimension 0, may hold values 0 or 1
- lengths: int32 [8], P('grp'), parts along dimension 0, may hold values from 1 to 6144, 15360 in all
- start_device: int32 [8], P('grp'), parts along dimension 0, may hold values from 0 to 3
- cache_latent: bfloat16 [8, 6144, 512], P('grp', 'blk'), parts along dimension 0, may hold values from -8 to 8
- cache_rope: bfloat16 [8, 64, 6144], P('grp', None, 'blk'), parts along dimension 0, may hold values from -8 to 8
- up_weight: bfloat16 [128, 512, 128], P('head'), may hold values from -1 to 1
Outputs:
- verified: bfloat16 [8, 32, 16384], P('grp', None, ('head', 'blk')), parts along dimension 0
There are 2 independent parts, one for each index of `grp`. A program takes and returns all parts, laid end to end along the dimension named above; an argument that names none is the same for every part. Nothing has to cross between parts.
Inputs may be any that keep to these rules, and one draw needn't show every extreme that they name: Together the lengths fill 5/8 of the cycle's slots; one request has exactly 6144 tokens. parents[r, 0] = 0; every other node's parent has a lower index.
All inputs are finite; a program needn't handle non-finite values.
Results may differ from a plain program's by a relative error of at most 0.012.
Values may be sent and summed in bfloat16 or wider, within the bound.
No kernel may reach another device: no remote copies, remote signals or barrier semaphores. Data moves between devices by JAX's collectives and lax.ppermute only.
A program may use at most 128 MiB of HBM per device.

v0:
```python
import functools
import math

import jax
import jax.numpy as jnp
from jax import lax
from jax.experimental import pallas as pl
from jax.experimental.pallas import tpu as pltpu
from jax.sharding import PartitionSpec as P

DN = 128

NEGATIVE = -1e30
STAT_ROWS = 16


def merged(value, axis, join):
    pieces = jax.tree.map(lambda part: lax.all_gather(part, axis), value)
    head = jax.tree.map(lambda part: part[0], pieces)
    tail = jax.tree.map(lambda part: part[1:], pieces)
    subtotal, _ = lax.scan(lambda subtotal, slab: (join(subtotal, slab), None), head, tail)
    return subtotal


def ancestor_matrix(parent_list):
    node_count = parent_list.shape[0]
    ordering = jnp.arange(node_count, dtype=jnp.int32)
    one_hop = (parent_list[:, None] == ordering[None, :]).astype(jnp.float32)
    reached = jnp.maximum(one_hop, jnp.eye(node_count, dtype=jnp.float32))
    for _ in range(max(node_count - 1, 1).bit_length()):
        reached = jnp.minimum(jnp.dot(reached, reached, precision=lax.Precision.HIGHEST), 1.0)
    return reached


def softmax_update(running, scores, visible, values):
    top_score, weight_sum, summed = running
    masked = jnp.where(visible, scores, -jnp.inf)
    new_top = jnp.maximum(top_score, jnp.max(masked, axis=1))
    factor = jnp.exp(top_score - new_top)
    expweights = jnp.exp(masked - new_top[:, None])
    summed = summed * factor[:, None] + jnp.dot(
        expweights.astype(jnp.bfloat16), values, preferred_element_type=jnp.float32
    )
    return (new_top, weight_sum * factor + jnp.sum(expweights, axis=1), summed)


def join_stats(first_stats, second_stats):
    top_one, sum_one = first_stats
    top_two, sum_two = second_stats
    top_both = jnp.maximum(top_one, top_two)
    return (top_both, sum_one * jnp.exp(top_one - top_both) + sum_two * jnp.exp(top_two - top_both))


def attend_page(running, query_block, lat_page, rope_page, live_count, score_scale):
    dim_lat = lat_page.shape[1]
    query_lat = query_block[:dim_lat]
    query_rope = query_block[dim_lat:]
    key_block = math.gcd(lat_page.shape[0], 512)

    def block_step(block_index, carried):
        first_key = block_index * key_block
        lat_rows = lax.dynamic_slice_in_dim(lat_page, first_key, key_block, 0)
        rope_rows = lax.dynamic_slice_in_dim(rope_page, first_key, key_block, 1)
        scores = lax.dot_general(
            query_lat, lat_rows, (((0,), (1,)), ((), ())), preferred_element_type=jnp.float32
        )
        scores = scores + lax.dot_general(
            query_rope, rope_rows, (((0,), (0,)), ((), ())), preferred_element_type=jnp.float32
        )
        scores = scores * score_scale
        visible = first_key + jnp.arange(key_block, dtype=jnp.int32) < live_count
        return softmax_update(carried, scores, visible[None, :], lat_rows)

    block_count = (live_count + key_block - 1) // key_block
    return lax.fori_loop(0, block_count, block_step, running)


def fresh_state(columns, dim_lat):
    return (
        jnp.full((columns,), NEGATIVE, jnp.float32),
        jnp.zeros((columns,), jnp.float32),
        jnp.zeros((columns, dim_lat), jnp.float32),
    )


def gathered_shards(
    queries,
    tree_keys,
    parents,
    node_live,
    lengths,
    start_device,
    cache_latent,
    cache_rope,
    up_weight,
):
    cycle_size = lax.axis_size("blk")
    position = lax.axis_index("blk")
    request_count = queries.shape[0]
    local_cols = queries.shape[2]
    node_count = tree_keys.shape[1]
    dim_lat = cache_latent.shape[2]
    dim_rope = cache_rope.shape[1]
    dim_value = up_weight.shape[2]
    page_rows = cache_latent.shape[1]
    own_heads = local_cols // node_count
    score_scale = 1.0 / math.sqrt(DN + dim_rope)
    page_index = (position - start_device) % cycle_size
    live_keys = jnp.clip(lengths - page_index * page_rows, 0, page_rows)
    piece = lax.all_gather(queries, "blk", axis=2, tiled=True)
    piece_cols = piece.shape[2]
    tops = []
    sums = []
    accs = []
    for fold_request in range(request_count):
        fold_outcome = attend_page(
            fresh_state(piece_cols, dim_lat),
            piece[fold_request],
            cache_latent[fold_request],
            cache_rope[fold_request],
            live_keys[fold_request],
            score_scale,
        )
        tops.append(fold_outcome[0])
        sums.append(fold_outcome[1])
        accs.append(fold_outcome[2])
    top_all = jnp.stack(tops)
    sum_all = jnp.stack(sums)
    acc_all = jnp.stack(accs)
    reached = jax.vmap(ancestor_matrix)(parents) > 0.5
    tree_tops, tree_sums, tree_accs = ([], [], [])
    for request in range(request_count):
        tree_scores = (
            lax.dot_general(
                queries[request],
                tree_keys[request],
                (((0,), (1,)), ((), ())),
                preferred_element_type=jnp.float32,
            )
            * score_scale
        )
        visible = jnp.tile(reached[request], (own_heads, 1))
        outcome = softmax_update(
            fresh_state(local_cols, dim_lat), tree_scores, visible, tree_keys[request][:, :dim_lat]
        )
        tree_tops.append(outcome[0])
        tree_sums.append(outcome[1])
        tree_accs.append(outcome[2])
    tree_top = jnp.stack(tree_tops)
    tree_sum = jnp.stack(tree_sums)
    tree_acc = jnp.stack(tree_accs)
    own_start = position * local_cols
    own_top = lax.dynamic_slice_in_dim(top_all, own_start, local_cols, 1)
    own_sum = lax.dynamic_slice_in_dim(sum_all, own_start, local_cols, 1)
    own_acc = lax.dynamic_slice_in_dim(acc_all, own_start, local_cols, 1)
    joined = jnp.maximum(own_top, tree_top)
    first_factor = jnp.exp(own_top - joined)
    second_factor = jnp.exp(tree_top - joined)
    top_all = lax.dynamic_update_slice_in_dim(top_all, joined, own_start, 1)
    sum_all = lax.dynamic_update_slice_in_dim(
        sum_all, own_sum * first_factor + tree_sum * second_factor, own_start, 1
    )
    acc_all = lax.dynamic_update_slice_in_dim(
        acc_all,
        own_acc * first_factor[:, :, None] + tree_acc * second_factor[:, :, None],
        own_start,
        1,
    )
    merged_top, merged_sum = merged((top_all, sum_all), "blk", join_stats)
    scaling = jnp.exp(top_all - merged_top) / merged_sum
    normed = acc_all * scaling[:, :, None]
    head_rows = lax.psum_scatter(
        normed.astype(jnp.bfloat16), "blk", scatter_dimension=1, tiled=True
    ).astype(jnp.float32)
    weight_own = lax.dynamic_slice_in_dim(up_weight, position * own_heads, own_heads, 0).astype(
        jnp.float32
    )
    projected = jnp.einsum(
        "rhnd,hdv->rnhv",
        head_rows.reshape(request_count, own_heads, node_count, dim_lat),
        weight_own,
        precision=lax.Precision.HIGHEST,
    )
    verified = projected.reshape(request_count, node_count, own_heads * dim_value)
    live_nodes = node_live.astype(jnp.float32)[:, :, None]
    return (verified * live_nodes).astype(jnp.bfloat16)


def dot_nn(left, right):
    return jnp.dot(left, right, preferred_element_type=jnp.float32)


def dot_tn(left, right):
    return lax.dot_general(
        left, right, (((0,), (0,)), ((), ())), preferred_element_type=jnp.float32
    )


def reach_closure(parent_row):
    count = parent_row.shape[1]
    row = lax.broadcasted_iota(jnp.int32, (count, count), 0)
    lane = lax.broadcasted_iota(jnp.int32, (count, count), 1)
    reached = jnp.where((row == parent_row) | (row == lane), 1.0, 0.0).astype(jnp.bfloat16)
    return reached


def page_softmax(query, lat_ref, rope_ref, page, keys, blocks, block, scale, score_ref, tree):
    dim_lat = lat_ref.shape[2]
    columns = query.shape[1]
    query_lat, query_rope = query[:dim_lat], query[dim_lat:]
    tops = []
    for index in range(blocks):
        span = slice(index * block, (index + 1) * block)
        scores = dot_nn(lat_ref[page, span, :], query_lat)
        scores = scores + dot_tn(rope_ref[page, :, span], query_rope)
        if index >= blocks - 2:
            place = index * block + lax.broadcasted_iota(jnp.int32, scores.shape, 0)
            scores = jnp.where(place < keys, scores, NEGATIVE)
        score_ref[span, :columns] = scores
        tops.append(jnp.max(scores, axis=0, keepdims=True))
    if tree is not None:
        tree_keys, visible = tree
        tree_scores = jnp.where(visible > 0.5, dot_nn(tree_keys, query), NEGATIVE)
        tops.append(jnp.max(tree_scores, axis=0, keepdims=True))
    top = functools.reduce(jnp.maximum, tops)
    base_two = scale * math.log2(math.e)
    shift = top * base_two
    total = summed = None
    for index in range(blocks):
        span = slice(index * block, (index + 1) * block)
        weights = jnp.exp2(score_ref[span, :columns] * base_two - shift)
        weight_sum = jnp.sum(weights, axis=0, keepdims=True)
        values = dot_tn(lat_ref[page, span, :], weights.astype(jnp.bfloat16))
        total = weight_sum if total is None else total + weight_sum
        summed = values if summed is None else summed + values
    if tree is not None:
        weights = jnp.exp2(tree_scores * base_two - shift)
        weight_sum = jnp.sum(weights, axis=0, keepdims=True)
        values = dot_tn(tree_keys[:, :dim_lat], weights.astype(jnp.bfloat16))
        total = weight_sum if total is None else total + weight_sum
        summed = values if summed is None else summed + values
    return summed, total, top * scale


class Book:
    def __init__(self, place_ref, length_ref, start_ref, page_rows):
        self.position, self.half = place_ref[0], place_ref[1]
        self.size = place_ref[2]
        self.lengths, self.starts = length_ref, start_ref
        self.page_rows = page_rows
        self.count = length_ref.shape[0]
        self.apart = shortest(length_ref)
        self.hub = ((self.position > 0) & (self.position < self.size - 1)).astype(jnp.int32)

    def request(self, place):
        moved = place + (place >= self.apart).astype(jnp.int32)
        return jnp.where(place == self.count - 1, self.apart, moved)

    def live(self, request, position):
        page = lax.rem(position - self.starts[request] + self.size, self.size)
        return jnp.clip(self.lengths[request] - page * self.page_rows, 0, self.page_rows)


def shortest(length_ref):
    best, index = length_ref[0], jnp.int32(0)
    for each in range(1, length_ref.shape[0]):
        less = length_ref[each] < best
        index = jnp.where(less, each, index)
        best = jnp.minimum(best, length_ref[each])
    return index


def sort_kernel(length_ref, query_ref, long_ref, apart_ref, held_ref, sems):
    apart = shortest(length_ref)
    most = long_ref.shape[0]
    stages = []
    for place in range(most + 1):
        if place < most:
            request, target = place + (place >= apart).astype(jnp.int32), long_ref.at[place]
        else:
            request, target = apart, apart_ref.at[0]
        held = held_ref.at[place]
        stages.append(
            (
                pltpu.make_async_copy(query_ref.at[request], held, sems.at[place, 0]),
                pltpu.make_async_copy(held, target, sems.at[place, 1]),
            )
        )
    for fetch, _ in stages:
        fetch.start()
    for fetch, put in stages:
        fetch.wait()
        put.start()
    for _, put in stages:
        put.wait()


def rope_pieces(half, width):
    return [(low, min(width, half - low)) for low in range(0, half, width)]


def pack_kernel(place_ref, length_ref, lat_ref, rope_ref, out_ref, sems):
    apart = shortest(length_ref)
    half = lat_ref.shape[1] // 2
    dim_rope = rope_ref.shape[1]
    width = lat_ref.shape[2]
    low = pl.multiple_of(place_ref[1] * half, 128)
    copies = [
        pltpu.make_async_copy(
            lat_ref.at[apart, pl.ds(low, half), :], out_ref.at[pl.ds(0, half), :], sems.at[0]
        )
    ]
    for index, (at, size) in enumerate(rope_pieces(half, width)):
        copies.append(
            pltpu.make_async_copy(
                rope_ref.at[apart, :, pl.ds(pl.multiple_of(low + at, 128), size)],
                out_ref.at[pl.ds(half + index * dim_rope, dim_rope), pl.ds(0, size)],
                sems.at[index + 1],
            )
        )
    for copy in copies:
        copy.start()
    for copy in copies:
        copy.wait()


def variants(keys, block_count, block, action):
    step = 2 if block_count % 2 == 0 else 1
    for blocks in range(step, block_count + 1, step):

        @pl.when((keys > (blocks - step) * block) & (keys <= blocks * block))
        def _():
            action(blocks)


def spans(place, nodes):
    if isinstance(place, int):
        return slice(place * nodes, (place + 1) * nodes), slice(place, place + 1)
    return pl.ds(pl.multiple_of(place * nodes, nodes), nodes), pl.ds(place, 1)


def store_value(rows_ref, level_ref, lane, place, nodes, summed, total, top):
    heads, _, dim_lat = rows_ref.shape[1:]
    span, line = spans(place, nodes)
    normed = (summed * (1.0 / total)).astype(jnp.bfloat16)
    rows_ref[lane, :, span, :] = normed.T.reshape(heads, nodes, dim_lat)
    level_ref[lane, line, :] = top + jnp.log(total)


def store_nothing(rows_ref, level_ref, lane, place, nodes):
    heads, _, dim_lat = rows_ref.shape[1:]
    span, line = spans(place, nodes)
    rows_ref[lane, :, span, :] = jnp.zeros((heads, nodes, dim_lat), jnp.bfloat16)
    level_ref[lane, line, :] = jnp.full((1, level_ref.shape[2]), NEGATIVE, jnp.float32)


def project(rows_ref, level_ref, weight_ref, lane, count, nodes, out_ref, stat_ref=None):
    heads = rows_ref.shape[1]
    columns, dim_value = level_ref.shape[2], weight_ref.shape[3]
    for head in range(heads):
        value = dot_nn(rows_ref[lane, head], weight_ref[lane, head])
        for each in range(count):
            piece = value[each * nodes : (each + 1) * nodes].astype(out_ref.dtype)
            out_ref[each, head * nodes : (head + 1) * nodes, :] = piece
    if stat_ref is not None:
        stat_ref[...] = level_ref[lane]
        return
    for each in range(count):
        out_ref[each, columns:, :] = level_rows(level_ref[lane, each : each + 1, :], dim_value)


def page_kernel(steps, own, block, scale, place_ref, length_ref, start_ref, *refs):
    refs = list(refs)
    query_hbm = [[refs.pop(0) for _ in group] for group in steps]
    if own:
        apart_hbm = refs.pop(0)
    lat_hbm, rope_hbm, weight_hbm = refs.pop(0), refs.pop(0), refs.pop(0)
    if own:
        tree_ref, parent_ref, part_ref, stat_ref = [refs.pop(0) for _ in range(4)]
        out_refs = [part_ref]
    else:
        out_refs = [refs.pop(0) for _ in steps]
    query_ref, lat_ref, rope_ref, weight_ref, rows_ref, level_ref, score_ref, reach_ref = refs[:8]
    page_sems, query_sems, weight_sems = refs[8:]
    page_rows = lat_ref.shape[1]
    book = Book(place_ref, length_ref, start_ref, page_rows)
    heads, columns = weight_ref.shape[1], level_ref.shape[2]
    nodes = columns // heads
    lanes = len(steps)
    count = book.count - (0 if own else 1)
    block_count = page_rows // block

    flags = []
    shards = []
    exist = []
    for group in steps:
        flag = shard = jnp.int32(0)
        each = []
        for step in group:
            there = book.position + step
            exists = ((there >= 0) & (there < book.size)).astype(jnp.int32)
            each.append(exists)
            flag = flag + exists
            shard = shard + exists * there
        flags.append(flag)
        shards.append(shard)
        exist.append(each)
    any_flag = jnp.minimum(functools.reduce(jnp.add, flags), 1)

    def keys_at(place):
        request = book.request(place)
        keys = book.live(request, book.position) * any_flag
        if own:
            keys = keys * jnp.where(place == count - 1, book.hub, 1)
        return request, keys

    def page_copies(place, request):
        return [
            pltpu.make_async_copy(lat_hbm.at[request], lat_ref.at[place], page_sems.at[place, 0]),
            pltpu.make_async_copy(rope_hbm.at[request], rope_ref.at[place], page_sems.at[place, 1]),
        ]

    def query_copy(ref, place, lane):
        target = query_ref.at[place, :, lane * columns : (lane + 1) * columns]
        return pltpu.make_async_copy(ref, target, query_sems.at[place, lane])

    def weight_copy(lane):
        low = pl.multiple_of(shards[lane] * heads, heads)
        return pltpu.make_async_copy(
            weight_hbm.at[pl.ds(low, heads)], weight_ref.at[lane], weight_sems.at[lane]
        )

    for place in range(count):
        request, keys = keys_at(jnp.int32(place))
        for lane, group in enumerate(query_hbm):
            for ref, exists in zip(group, exist[lane]):
                source = apart_hbm.at[0] if own and place == count - 1 else ref.at[place]

                @pl.when(exists * (keys + int(own)) > 0)
                def _():
                    query_copy(source, place, lane).start()

        @pl.when(keys > 0)
        def _():
            for copy in page_copies(place, request):
                copy.start()

    for lane in range(lanes):

        @pl.when(flags[lane] > 0)
        def _():
            weight_copy(lane).start()

    if own:
        reached = reach_closure(parent_ref[...])
        for _ in range(max(nodes - 1, 1).bit_length()):
            reached = jnp.minimum(dot_nn(reached, reached), 1.0).astype(jnp.bfloat16)
        reach_ref[...] = reached.astype(jnp.float32)

    def item_step(place, carry):
        request, keys = keys_at(place)
        for lane, group in enumerate(query_hbm):

            @pl.when(flags[lane] * (keys + int(own)) > 0)
            def _():
                query_copy(group[0].at[0], place, lane).wait()

        @pl.when(keys > 0)
        def _():
            for copy in page_copies(place, request):
                copy.wait()

        def attend(blocks, query):
            tree = None
            if own:
                base = pl.multiple_of(request * nodes, nodes)
                row = lax.broadcasted_iota(jnp.int32, (reach_ref.shape[1], columns), 0)
                along = lax.broadcasted_iota(jnp.int32, (reach_ref.shape[1], columns), 1)
                pick = jnp.where(row == base + along % nodes, 1.0, 0.0).astype(jnp.bfloat16)
                near = reach_ref[pl.ds(base, nodes), :].astype(jnp.bfloat16)
                tree = (tree_ref[request], dot_nn(near, pick))
            return page_softmax(
                query, lat_ref, rope_ref, place, keys, blocks, block, scale, score_ref, tree
            )

        def attend_one(lane):
            def action(blocks):
                if isinstance(lane, int):
                    query = query_ref[place, :, lane * columns : (lane + 1) * columns]
                else:
                    query = query_ref[place, :, pl.ds(pl.multiple_of(lane * columns, columns), columns)]
                store_value(rows_ref, level_ref, lane, place, nodes, *attend(blocks, query))

            return action

        def attend_all(blocks):
            summed, total, top = attend(blocks, query_ref[place])
            for lane in range(lanes):
                span = slice(lane * columns, (lane + 1) * columns)
                store_value(
                    rows_ref, level_ref, lane, place, nodes, summed[:, span], total[:, span], top[:, span]
                )

        if lanes == 1:
            variants(keys, block_count, block, attend_one(0))
        else:
            together = functools.reduce(jnp.multiply, flags)
            alone = functools.reduce(
                jnp.add, [lane * flag for lane, flag in enumerate(flags)]
            ) * (1 - together)
            variants(keys * together, block_count, block, attend_all)
            variants(keys * (1 - together), block_count, block, attend_one(alone))

        @pl.when(keys <= 0)
        def _():
            if own:
                attend_one(0)(0)
            else:
                for lane in range(lanes):
                    store_nothing(rows_ref, level_ref, lane, place, nodes)

        return carry

    lax.fori_loop(0, count * any_flag, item_step, 0)
    for lane in range(lanes):

        @pl.when(flags[lane] > 0)
        def _():
            weight_copy(lane).wait()
            project(
                rows_ref, level_ref, weight_ref, lane, count, nodes, out_refs[lane],
                stat_ref if own else None,
            )


def hub_kernel(block, scale, place_ref, length_ref, start_ref, *refs):
    refs = list(refs)
    query_hbm = [refs.pop(0) for _ in range(4)]
    mine_hbm, other_hbm, lat_hbm, rope_hbm, weight_hbm = [refs.pop(0) for _ in range(5)]
    out_refs = [refs.pop(0) for _ in range(3)]
    part_ref, stat_ref = refs.pop(0), refs.pop(0)
    query_ref, lat_ref, rope_ref, weight_ref, rows_ref, level_ref, score_ref = refs[:7]
    sum_ref, acc_ref, query_sems, page_sems, end_sems, weight_sems = refs[7:]
    page_rows, dim_lat = lat_ref.shape[1:]
    dim_rope = rope_ref.shape[1]
    book = Book(place_ref, length_ref, start_ref, page_rows)
    heads, columns = weight_ref.shape[1], level_ref.shape[2]
    nodes = columns // heads
    half = page_rows // 2
    block_count = page_rows // block
    request = book.apart
    low_side = book.position * 2 < book.size
    end = jnp.where(low_side, 0, book.size - 1)
    far = jnp.where(low_side, book.position + 2, book.position - 2)
    shards = [book.position - 1, book.position + 1, far, book.position]
    live = [book.live(request, book.position), book.live(request, end)]

    @pl.when(book.hub == 0)
    def _():
        nothing = level_rows(jnp.full((1, columns), NEGATIVE, jnp.float32), part_ref.shape[2])
        for out_ref in out_refs:
            out_ref[0, :columns, :] = jnp.zeros((columns, out_ref.shape[2]), out_ref.dtype)
            out_ref[0, columns:, :] = nothing
        part_ref[...] = jnp.zeros_like(part_ref)
        stat_ref[...] = jnp.full_like(stat_ref, NEGATIVE)

    @pl.when(book.hub > 0)
    def _():
        copies = [
            pltpu.make_async_copy(
                ref.at[0],
                query_ref.at[lane // 2, :, lane % 2 * columns : (lane % 2 + 1) * columns],
                query_sems.at[lane],
            )
            for lane, ref in enumerate(query_hbm)
        ]
        copies.append(pltpu.make_async_copy(lat_hbm.at[request], lat_ref.at[0], page_sems.at[0]))
        copies.append(pltpu.make_async_copy(rope_hbm.at[request], rope_ref.at[0], page_sems.at[1]))
        at_sem = 0
        for ref, part in ((mine_hbm, book.half), (other_hbm, 1 - book.half)):
            low = pl.multiple_of(part * half, 128)
            copies.append(
                pltpu.make_async_copy(
                    ref.at[pl.ds(0, half), :], lat_ref.at[1, pl.ds(low, half), :], end_sems.at[at_sem]
                )
            )
            at_sem += 1
            for index, (at, size) in enumerate(rope_pieces(half, dim_lat)):
                copies.append(
                    pltpu.make_async_copy(
                        ref.at[pl.ds(half + index * dim_rope, dim_rope), pl.ds(0, size)],
                        rope_ref.at[1, :, pl.ds(pl.multiple_of(low + at, 128), size)],
                        end_sems.at[at_sem],
                    )
                )
                at_sem += 1
        weight_copies = [
            pltpu.make_async_copy(
                weight_hbm.at[pl.ds(pl.multiple_of(shard * heads, heads), heads)],
                weight_ref.at[lane],
                weight_sems.at[lane],
            )
            for lane, shard in enumerate(shards)
        ]
        for copy in copies + weight_copies:
            copy.start()
        for copy in copies:
            copy.wait()

        def group_step(item, carry):
            group, page = lax.div(item, 2), lax.rem(item, 2)
            keys = jnp.where(page == 0, live[0], live[1])
            narrow = (group == 1) & (page == 0)

            @pl.when(page == 0)
            def _():
                sum_ref[0:1, :] = jnp.zeros((1, 2 * columns), jnp.float32)
                sum_ref[1:2, :] = jnp.full((1, 2 * columns), NEGATIVE, jnp.float32)
                acc_ref[...] = jnp.zeros_like(acc_ref)

            def attend(width):
                def action(blocks):
                    summed, total, top = page_softmax(
                        query_ref[group, :, :width], lat_ref, rope_ref, page, keys, blocks, block, scale,
                        score_ref, None,
                    )
                    old_top = sum_ref[1:2, :width]
                    new_top = jnp.maximum(old_top, top)
                    old_share, new_share = jnp.exp(old_top - new_top), jnp.exp(top - new_top)
                    sum_ref[0:1, :width] = sum_ref[0:1, :width] * old_share + total * new_share
                    sum_ref[1:2, :width] = new_top
                    acc_ref[:, :width] = acc_ref[:, :width] * old_share + summed * new_share

                return action

            variants(jnp.where(narrow, 0, keys), block_count, block, attend(2 * columns))
            variants(jnp.where(narrow, keys, 0), block_count, block, attend(columns))

            @pl.when(page == 1)
            def _():
                for side in range(2):
                    lane = group * 2 + side
                    span = slice(side * columns, (side + 1) * columns)
                    some = live[1] + (live[0] if side == 0 else jnp.where(group == 1, 0, live[0]))

                    @pl.when(some > 0)
                    def _():
                        outcome = acc_ref[:, span], sum_ref[0:1, span], sum_ref[1:2, span]
                        store_value(rows_ref, level_ref, lane, 0, nodes, *outcome)

                    @pl.when(some <= 0)
                    def _():
                        store_nothing(rows_ref, level_ref, lane, 0, nodes)

            return carry

        lax.fori_loop(0, 4, group_step, 0)
        for copy in weight_copies:
            copy.wait()
        outer = jnp.where(low_side, 0, 1)
        for lane, out_ref in zip((outer, 1 - outer, 2), out_refs):
            project(rows_ref, level_ref, weight_ref, lane, 1, nodes, out_ref)
        project(rows_ref, level_ref, weight_ref, 3, 1, nodes, part_ref, stat_ref)


def level_rows(level, lanes):
    pieces = []
    rest = level
    for _ in range(3):
        piece = rest.astype(jnp.bfloat16).astype(jnp.float32)
        rest = rest - piece
        pieces.append(piece)
    rows = [
        piece[:, first : first + lanes] for piece in pieces for first in range(0, level.shape[1], lanes)
    ]
    rows.append(jnp.zeros((STAT_ROWS - len(rows), lanes), jnp.float32))
    return jnp.concatenate(rows, axis=0).astype(jnp.bfloat16)


def level_row(block, columns):
    per = columns // block.shape[1]
    block = block.astype(jnp.float32)
    return jnp.concatenate(
        [block[i : i + 1] + block[per + i : per + i + 1] + block[2 * per + i : 2 * per + i + 1] for i in range(per)],
        axis=1,
    )


def merge_kernel(layout, heads, place_ref, length_ref, start_ref, part_ref, stat_ref, live_ref,
                 apart_ref, apart_stat_ref, *refs):
    book = Book(place_ref, length_ref, start_ref, 1)
    request_count, columns, dim_value = part_ref.shape
    nodes = columns // heads
    remote_refs, out_ref = refs[: len(layout)], refs[len(layout)]
    nothing = jnp.full((1, columns), NEGATIVE, jnp.float32)
    requests = [book.request(jnp.int32(place)) for place in range(request_count)]
    levels = [[stat_ref[place : place + 1, :]] for place in range(request_count)]
    values = [[part_ref[place]] for place in range(request_count)]
    for kind, ref in zip(layout, remote_refs):
        if isinstance(kind, bool):
            exists = book.hub == int(kind)
        else:
            exists = functools.reduce(
                jnp.logical_or,
                [(book.position + step >= 0) & (book.position + step < book.size) for step in kind],
            )
        first = request_count - 1 if isinstance(kind, bool) else 0
        for each in range(ref.shape[0]):
            level = level_row(ref[each, columns:, :], columns)
            levels[first + each].append(jnp.where(exists, level, NEGATIVE))
            values[first + each].append(ref[each, :columns, :].astype(jnp.float32))
    levels[-1].append(apart_stat_ref[...])
    values[-1].append(apart_ref[0])
    rows = []
    for request, request_levels in zip(requests, levels):
        top = functools.reduce(jnp.maximum, request_levels)
        weights = [jnp.exp(level - top) for level in request_levels]
        total = live_ref[pl.ds(request, 1), :] / functools.reduce(jnp.add, weights)
        rows += [weight * total for weight in weights]
    rows += [nothing] * (-len(rows) % 8)
    shares = jnp.concatenate(rows, axis=0).T
    at = 0
    for request, request_values in zip(requests, values):
        value = None
        for each in request_values:
            term = each * shares[:, at : at + 1]
            value = term if value is None else value + term
            at += 1
        for head in range(heads):
            piece = value[head * nodes : (head + 1) * nodes].astype(jnp.bfloat16)
            out_ref[request, :, head * dim_value : (head + 1) * dim_value] = piece


VMEM = pl.BlockSpec(memory_space=pltpu.VMEM)
SMEM = pl.BlockSpec(memory_space=pltpu.SMEM)
HBM = pl.BlockSpec(memory_space=pltpu.HBM)
VMEM_LIMIT = 57 << 20


def call(kernel, operands, out_shapes, scratch, flops=0, limit=VMEM_LIMIT, out_space=VMEM):
    return pl.pallas_call(
        kernel,
        in_specs=[spec for spec, _ in operands],
        out_specs=[out_space] * len(out_shapes),
        scratch_shapes=scratch,
        out_shape=[jax.ShapeDtypeStruct(shape, dtype) for shape, dtype in out_shapes],
        compiler_params=pltpu.CompilerParams(vmem_limit_bytes=limit),
        cost_estimate=pl.CostEstimate(flops=flops, bytes_accessed=flops // 256, transcendentals=0),
    )(*[array for _, array in operands])


def after(value, *others):
    return lax.optimization_barrier((value, *others))[0]


def hub_shards(
    queries,
    tree_keys,
    parents,
    node_live,
    lengths,
    start_device,
    cache_latent,
    cache_rope,
    up_weight,
):
    size = lax.axis_size("blk")
    head_size = lax.axis_size("head")
    request_count, width, columns = queries.shape
    page_rows, dim_lat = cache_latent.shape[1:]
    dim_rope = cache_rope.shape[1]
    dim_value = up_weight.shape[2]
    heads = up_weight.shape[0] // size
    nodes = columns // heads
    rows = columns + STAT_ROWS
    block = math.gcd(page_rows, 256)
    scale = 1.0 / math.sqrt(DN + dim_rope)
    most = request_count - 1
    bf16, f32 = jnp.bfloat16, jnp.float32
    dma = pltpu.SemaphoreType.DMA
    position = lax.axis_index("blk")
    here = jnp.stack([position, lax.axis_index("head") % 2, jnp.int32(size)]).astype(jnp.int32)
    scalars = [(SMEM, here), (SMEM, lengths), (SMEM, start_device)]
    pages = [(HBM, cache_latent), (HBM, cache_rope), (HBM, up_weight)]
    unit_flops = 2 * columns * page_rows * (width + dim_lat)

    long, apart = call(
        sort_kernel,
        [(SMEM, lengths), (HBM, queries)],
        [((most, width, columns), bf16), ((1, width, columns), bf16)],
        [pltpu.VMEM((request_count, width, columns), bf16), dma((request_count, 2))],
        out_space=HBM,
    )
    half = page_rows // 2
    pieces = rope_pieces(half, dim_lat)

    def answer(steps, query_groups, own=(), space=HBM, limit=VMEM_LIMIT):
        lanes = len(steps)
        count = request_count if own else most
        operands = scalars + [(space, query) for group in query_groups for query in group]
        if own:
            operands += [(HBM, own[0])]
        operands += pages
        if own:
            operands += [(VMEM, array) for array in own[1:]]
            outs = [((count, columns, dim_value), f32), ((count, columns), f32)]
        else:
            outs = [((count, rows, dim_value), bf16)] * lanes
        reach_size = request_count * nodes if own else 8
        return call(
            functools.partial(page_kernel, steps, bool(own), block, scale),
            operands,
            outs,
            [
                pltpu.VMEM((count, width, lanes * columns), bf16),
                pltpu.VMEM((count, page_rows, dim_lat), bf16),
                pltpu.VMEM((count, dim_rope, page_rows), bf16),
                pltpu.VMEM((lanes, heads, dim_lat, dim_value), bf16),
                pltpu.VMEM((lanes, heads, count * nodes, dim_lat), bf16),
                pltpu.VMEM((lanes, count, columns), f32),
                pltpu.VMEM((page_rows, lanes * columns), f32),
                pltpu.VMEM((reach_size, reach_size), f32),
                dma((count, 2)),
                dma((count, lanes)),
                dma((lanes,)),
            ],
            unit_flops * lanes * count,
            limit,
        )

    def shift(value, pairs):
        return lax.ppermute(value, "blk", pairs)

    right1 = shift(long, [(i, i + 1) for i in range(size - 1)])
    left1 = shift(long, [(i, i - 1) for i in range(1, size)])
    apart_right = shift(apart, [(i, i + 1) for i in range(size - 2)])
    apart_left = shift(apart, [(i, i - 1) for i in range(2, size)])
    parent_row = (parents + nodes * jnp.arange(request_count, dtype=jnp.int32)[:, None]).reshape(1, -1)
    live_rows = jnp.tile(node_live.astype(f32), (1, heads))
    part, stat = answer([[0]], [[long]], (apart, tree_keys, parent_row))
    right2 = shift(after(right1, part), [(i, i + 1) for i in range(1, size - 1)])
    left2 = shift(after(left1, part), [(i, i - 1) for i in range(1, size - 1)])
    (packed,) = call(
        pack_kernel,
        [(SMEM, here), (SMEM, after(lengths, right1, left1)), (HBM, cache_latent), (HBM, cache_rope)],
        [((half + len(pieces) * dim_rope, dim_lat), bf16)],
        [dma((1 + len(pieces),))],
    )
    mine = shift(packed, [(0, 1), (size - 1, size - 2)])
    first = answer([[-1], [1]], [[after(right1, apart_right, apart_left)], [left1]])
    from_right = shift(first[0], [(i, i - 1) for i in range(1, size)])
    from_left = shift(first[1], [(i, i + 1) for i in range(size - 1)])
    swapped = lax.ppermute(
        after(mine, *first),
        ("blk", "head"),
        [(i * head_size + j, i * head_size + (j ^ 1)) for i in (1, size - 2) for j in range(head_size)],
    )
    crossing = jnp.where(position * 2 < size, apart_right, apart_left)
    apart_far = shift(after(crossing, *first), [(1, size - 2), (size - 2, 1)])
    right3 = shift(after(right2, *first), [(size - 2, size - 1)])
    left3 = shift(after(left2, *first), [(1, 0)])
    (second,) = answer([[-2, 2]], [[after(right2, from_right, from_left), left2]])
    from_far = shift(second, [(i, i - 2) for i in range(2, size)] + [(i, i + 2) for i in range(size - 2)])
    outer, inner, distant, apart_part, apart_stat = call(
        functools.partial(hub_kernel, block, scale),
        scalars
        + [
            (HBM, array)
            for array in (
                apart_right, apart_left, after(apart_far, second), apart, mine, swapped
            )
        ]
        + pages,
        [((1, rows, dim_value), bf16)] * 3 + [((1, columns, dim_value), f32), ((1, columns), f32)],
        [
            pltpu.VMEM((2, width, 2 * columns), bf16),
            pltpu.VMEM((2, page_rows, dim_lat), bf16),
            pltpu.VMEM((2, dim_rope, page_rows), bf16),
            pltpu.VMEM((4, heads, dim_lat, dim_value), bf16),
            pltpu.VMEM((4, heads, nodes, dim_lat), bf16),
            pltpu.VMEM((4, 1, columns), f32),
            pltpu.VMEM((page_rows, 2 * columns), f32),
            pltpu.VMEM((8, 2 * columns), f32),
            pltpu.VMEM((dim_lat, 2 * columns), f32),
            dma((4,)),
            dma((2,)),
            dma((2 * (1 + len(pieces)),)),
            dma((4,)),
        ],
        unit_flops * 7,
    )
    from_hub = shift(outer, [(1, 0), (size - 2, size - 1)])
    from_other = shift(inner, [(1, size - 2), (size - 2, 1)])
    from_distant = shift(distant, [(size - 2, 0), (1, size - 1)])
    (third,) = answer(
        [[1 - size, size - 1]], [[after(right3, outer, from_far), left3]], space=VMEM, limit=44 << 20
    )
    from_end = shift(third, [(0, size - 1), (size - 1, 0)])
    layout = [[1], [-1], [-2, 2], [1 - size, size - 1], False, True, False]
    arrays = (
        part, stat, live_rows, apart_part, apart_stat, from_right, from_left, from_far, from_end,
        from_hub, from_other, from_distant,
    )
    (verified,) = call(
        functools.partial(merge_kernel, layout, heads),
        scalars + [(VMEM, array) for array in arrays],
        [((request_count, nodes, heads * dim_value), bf16)],
        [],
        limit=12 << 20,
    )
    return verified


def solution(mesh):
    size = mesh.shape["blk"]
    hubs = size == 4 and mesh.shape["head"] % 2 == 0

    def shards(queries, *rest):
        columns = queries.shape[2]
        cache_latent, _, up_weight = rest[-3:]
        wide = columns % up_weight.shape[2] == 0 and cache_latent.shape[1] % 256 == 0
        if hubs and wide and queries.shape[0] > 1:
            return hub_shards(queries, *rest)
        return gathered_shards(queries, *rest)

    return jax.shard_map(
        shards,
        mesh=mesh,
        in_specs=(
            P("grp", None, ("head", "blk")),
            P("grp", None, None),
            P("grp", None),
            P("grp", None),
            P("grp"),
            P("grp"),
            P("grp", "blk", None),
            P("grp", None, "blk"),
            P("head", None, None),
        ),
        out_specs=P("grp", None, ("head", "blk")),
        check_vma=False,
    )
```

profile of v0, /device:TPU:0, one launch (start us, length us, event | category | flops | bytes accessed | tf_op | source)
XLA Modules:
  0.0 135.0 jit_solution(8675930634882752452)
XLA Ops:
  0.0 2.7 %shard_map.91 = (bf16[3,576,256]{2,1,0:T(8,128)(2,1)}, bf16[1,576,256]{2,1,0:T(8,128)(2,1)}) custom-call(s32[4]{0:T(128)} %length_ref.14, bf16[4,576,256]{2,1,0:T(8,128)(2,1)} %query_ref.1), custom_call_target="tpu_custom_call" | custom-call | tf_op jit(solution)/shard_map/pallas_call | solution.py:741
  2.7 1.3 collective-permute-start.3
  4.0 5.6 %collective-permute-start.2 = (bf16[3,576,256]{2,1,0:T(8,128)(2,1)}, bf16[3,576,256]{2,1,0:T(8,128)(2,1)S(1)}, u32[]{:S(2)}, u32[]{:S(2)}) collective-permute-start(bf16[3,576,256]{2,1,0:T(8,128)(2,1)} %get-tuple-element.27.refs_0_), channel_id=1, source_target_pairs={{0,4},{4,8},{8,12},{1,5},{5,9},{9,13},{2,6},{6,10},{10,14},{3,7},{... | collective-permute-start | bytes 2654216 | tf_op jit(solution)/shard_map/ppermute | solution.py:832
  9.7 0.7 collective-permute-start.1
  10.4 4.5 %collective-permute-start = (bf16[1,576,256]{2,1,0:T(8,128)(2,1)}, bf16[1,576,256]{2,1,0:T(8,128)(2,1)S(1)}, u32[]{:S(2)}, u32[]{:S(2)}) collective-permute-start(bf16[1,576,256]{2,1,0:T(8,128)(2,1)} %get-tuple-element.28.refs_1_.refs_3_), channel_id=1, source_target_pairs={{0,4},{4,8},{1,5},{5,9},{2,6},{6,10},{3,7},{7,11},{16,20},{20,24},... | collective-permute-start | bytes 884744 | tf_op jit(solution)/shard_map/ppermute | solution.py:832
  14.9 0.7 pad_add_fusion.place_ref
  15.6 12.0 %collective-permute-done.3.refs_1_ = bf16[3,576,256]{2,1,0:T(8,128)(2,1)S(1)} collective-permute-done((bf16[3,576,256]{2,1,0:T(8,128)(2,1)}, bf16[3,576,256]{2,1,0:T(8,128)(2,1)S(1)}, u32[]{:S(2)}, u32[]{:S(2)}) %collective-permute-start.3) | collective-permute-done | bytes 884768 | tf_op jit(solution)/shard_map/ppermute | solution.py:832
  27.6 2.4 %collective-permute-done.2.refs_0_ = bf16[3,576,256]{2,1,0:T(8,128)(2,1)S(1)} collective-permute-done((bf16[3,576,256]{2,1,0:T(8,128)(2,1)}, bf16[3,576,256]{2,1,0:T(8,128)(2,1)S(1)}, u32[]{:S(2)}, u32[]{:S(2)}) %collective-permute-start.2) | collective-permute-done | bytes 884768 | tf_op jit(solution)/shard_map/ppermute | solution.py:832
  30.0 2.8 %shard_map.95 = bf16[896,512]{1,0:T(8,128)(2,1)} custom-call(s32[3]{0:T(128)} %pad_add_fusion.place_ref, s32[4]{0:T(128)} %length_ref.14, bf16[4,1536,512]{2,1,0:T(8,128)(2,1)} %refs_2_.7, bf16[4,64,1536]{2,1,0:T(8,128)(2,1)} %refs_3_.7), custom_call_target="tpu_custom_call" | custom-call | tf_op jit(solution)/shard_map/pallas_call | solution.py:741
  32.7 5.2 %collective-permute-start.9 = (bf16[896,512]{1,0:T(8,128)(2,1)}, bf16[896,512]{1,0:T(8,128)(2,1)}, u32[]{:S(2)}, u32[]{:S(2)}) collective-permute-start(bf16[896,512]{1,0:T(8,128)(2,1)} %shard_map.95), channel_id=1, source_target_pairs={{0,4},{12,8},{1,5},{13,9},{2,6},{14,10},{3,7},{15,11},{16,20},{28,... | collective-permute-start | bytes 2752520 | tf_op jit(solution)/shard_map/ppermute | solution.py:832
  38.6 10.6 %shard_map.92 = (f32[4,256,128]{2,1,0:T(8,128)}, f32[4,256]{1,0:T(4,128)}) custom-call(s32[3]{0:T(128)} %pad_add_fusion.place_ref, s32[4]{0:T(128)} %length_ref.14, s32[4]{0:T(128)} %start_ref.11, bf16[3,576,256]{2,1,0:T(8,128)(2,1)} %get-tuple-element.27.refs_0_, bf16[1,576,256]{2,1,0:T(8,128)(2,1)} %get-tuple-element.28.refs_1_.refs_3_, ...), custom_call_target="tpu_custom_call" | custom-call | flops 3422552064 | bytes 13369344 | tf_op jit(solution)/shard_map/pallas_call | solution.py:741
  49.2 1.3 collective-permute-start.8
  50.5 1.6 %collective-permute-start.5 = (bf16[3,576,256]{2,1,0:T(8,128)(2,1)S(1)}, bf16[3,576,256]{2,1,0:T(8,128)(2,1)}, u32[]{:S(2)}, u32[]{:S(2)}) collective-permute-start(bf16[3,576,256]{2,1,0:T(8,128)(2,1)S(1)} %collective-permute-done.2.refs_0_), channel_id=1, source_target_pairs={{4,8},{8,12},{5,9},{9,13},{6,10},{10,14},{7,11},{11,15},{20,24},{2... | collective-permute-start | bytes 2654216 | tf_op jit(solution)/shard_map/ppermute | solution.py:832
  52.1 8.5 %shard_map.93 = (bf16[3,272,128]{2,1,0:T(8,128)(2,1)}, bf16[3,272,128]{2,1,0:T(8,128)(2,1)}) custom-call(s32[3]{0:T(128)} %pad_add_fusion.place_ref, s32[4]{0:T(128)} %length_ref.14, s32[4]{0:T(128)} %start_ref.11, bf16[3,576,256]{2,1,0:T(8,128)(2,1)} %copy-done.22, bf16[3,576,256]{2,1,0:T(8,128)(2,1)} %copy-done.23, bf16[4,1536,512]{2,1,0:T(8,128)(2,1)} %refs_2_.7, ...), custom_call_target="tpu_custom_call" | custom-call | flops 5133828096 | bytes 20054016 | tf_op jit(solution)/shard_map/pallas_call | solution.py:741
  60.7 1.6 %collective-permute-start.10 = (bf16[896,512]{1,0:T(8,128)(2,1)}, bf16[896,512]{1,0:T(8,128)(2,1)}, u32[]{:S(2)}, u32[]{:S(2)}) collective-permute-start(bf16[896,512]{1,0:T(8,128)(2,1)} %collective-permute-done.9.refs_4_), channel_id=1, source_target_pairs={{4,5},{5,4},{6,7},{7,6},{8,9},{9,8},{10,11},{11,10},{20,21},{21,20... | collective-permute-start | bytes 2752520 | tf_op jit(solution)/shard_map/ppermute | solution.py:853
  62.3 1.3 collective-permute-start.6
  63.6 10.3 %collective-permute-start.7 = (bf16[3,272,128]{2,1,0:T(8,128)(2,1)}, bf16[3,272,128]{2,1,0:T(8,128)(2,1)S(1)}, u32[]{:S(2)}, u32[]{:S(2)}) collective-permute-start(bf16[3,272,128]{2,1,0:T(8,128)(2,1)} %get-tuple-element.33), channel_id=1, source_target_pairs={{0,4},{4,8},{8,12},{1,5},{5,9},{9,13},{2,6},{6,10},{10,14},{3,7},{... | collective-permute-start | bytes 626696 | tf_op jit(solution)/shard_map/ppermute | solution.py:832
  73.9 1.3 collective-permute-start.13
  75.2 0.7 collective-permute-start.12
  76.0 0.7 broadcast_select_fusion
  76.7 1.3 collective-permute-done.6.refs_0_
  78.0 0.7 copy-done.3
  78.7 0.7 collective-permute-start.4
  79.4 0.7 copy-done.5
  80.1 8.3 %shard_map.94 = bf16[3,272,128]{2,1,0:T(8,128)(2,1)} custom-call(s32[3]{0:T(128)} %pad_add_fusion.place_ref, s32[4]{0:T(128)} %length_ref.14, s32[4]{0:T(128)} %start_ref.11, bf16[3,576,256]{2,1,0:T(8,128)(2,1)} %collective-permute-done.5.refs_0_, bf16[3,576,256]{2,1,0:T(8,128)(2,1)} %collective-permute-done.8.refs_1_, bf16[4,1536,512]{2,1,0:T(8,128)(2,1)} %refs_2_.7, ...), custom_call_target="tpu_custom_call" | custom-call | flops 2566914048 | bytes 10027008 | tf_op jit(solution)/shard_map/pallas_call | solution.py:741
  88.4 2.9 %collective-permute-start.11 = (bf16[3,272,128]{2,1,0:T(8,128)(2,1)}, bf16[3,272,128]{2,1,0:T(8,128)(2,1)S(1)}, u32[]{:S(2)}, u32[]{:S(2)}) collective-permute-start(bf16[3,272,128]{2,1,0:T(8,128)(2,1)} %shard_map.94), channel_id=1, source_target_pairs={{8,0},{12,4},{0,8},{4,12},{9,1},{13,5},{1,9},{5,13},{10,2},{14,6},... | collective-permute-start | bytes 626696 | tf_op jit(solution)/shard_map/ppermute | solution.py:832
  91.3 0.7 copy-done.24
  92.0 1.8 %shard_map.96 = (bf16[1,272,128]{2,1,0:T(8,128)(2,1)}, bf16[1,272,128]{2,1,0:T(8,128)(2,1)}, bf16[1,272,128]{2,1,0:T(8,128)(2,1)}, f32[1,256,128]{2,1,0:T(8,128)}, f32[1,256]{1,0:T(1,128)}) custom-call(s32[3]{0:T(128)} %pad_add_fusion.place_ref, s32[4]{0:T(128)} %length_ref.14, s32[4]{0:T(128)} %start_ref.11, bf16[1,576,256]{2,1,0:T(8,128)(2,1)} %copy-done.19, ...), custom_call_target="tpu_custom_call" | custom-call | flops 5989466112 | bytes 23396352 | tf_op jit(solution)/shard_map/pallas_call | solution.py:741
  93.9 7.3 %collective-permute-done.11.refs_2_ = bf16[3,272,128]{2,1,0:T(8,128)(2,1)S(1)} collective-permute-done((bf16[3,272,128]{2,1,0:T(8,128)(2,1)}, bf16[3,272,128]{2,1,0:T(8,128)(2,1)S(1)}, u32[]{:S(2)}, u32[]{:S(2)}) %collective-permute-start.11) | collective-permute-done | bytes 208928 | tf_op jit(solution)/shard_map/ppermute | solution.py:832
  101.2 0.7 copy-done.7
  102.3 0.7 copy-done.10
  102.9 0.7 copy-done.12
  103.6 0.7 copy-done.14
  104.3 8.2 %shard_map.97 = bf16[3,272,128]{2,1,0:T(8,128)(2,1)} custom-call(s32[3]{0:T(128)S(1)} %copy-done.12, s32[4]{0:T(128)S(1)} %copy-done.10, s32[4]{0:T(128)S(1)} %copy-done.14, bf16[3,576,256]{2,1,0:T(8,128)(2,1)S(1)} %collective-permute-done.12.refs_0_, bf16[3,576,256]{2,1,0:T(8,128)(2,1)S(1)} %collective-permute-done.13.refs_1_, ...), custom_call_target="tpu_custom_call" | custom-call | flops 2566914048 | bytes 10027008 | tf_op jit(solution)/shard_map/pallas_call | solution.py:741
  112.5 4.1 %collective-permute-start.14 = (bf16[3,272,128]{2,1,0:T(8,128)(2,1)}, bf16[3,272,128]{2,1,0:T(8,128)(2,1)S(1)}, u32[]{:S(2)}, u32[]{:S(2)}) collective-permute-start(bf16[3,272,128]{2,1,0:T(8,128)(2,1)} %shard_map.97), channel_id=1, source_target_pairs={{0,12},{12,0},{1,13},{13,1},{2,14},{14,2},{3,15},{15,3},{16,28},{2... | collective-permute-start | bytes 626696 | tf_op jit(solution)/shard_map/ppermute | solution.py:832
  116.5 0.7 collective-permute-start.16
  117.2 1.3 collective-permute-start.17
  118.5 1.3 collective-permute-start.15
  119.9 4.6 %collective-permute-done.17.refs_6_ = bf16[1,272,128]{2,1,0:T(8,128)(2,1)S(1)} collective-permute-done((bf16[1,272,128]{2,1,0:T(8,128)(2,1)}, bf16[1,272,128]{2,1,0:T(8,128)(2,1)S(1)}, u32[]{:S(2)}, u32[]{:S(2)}) %collective-permute-start.17) | collective-permute-done | bytes 69664 | tf_op jit(solution)/shard_map/ppermute | solution.py:832
  124.5 1.2 collective-permute-done.15.refs_4_
  125.8 0.9 copy-done.4
  126.7 0.9 copy-done.6
  127.6 0.9 copy-done.8
  128.6 0.9 copy-done.9
  130.1 0.7 copy-done.13
  131.4 0.7 copy-done.16
  132.1 0.7 copy-done.17
  132.8 2.2 %shard_map.98 = bf16[4,32,1024]{2,1,0:T(8,128)(2,1)} custom-call(s32[3]{0:T(128)S(1)} %copy-done.13, s32[4]{0:T(128)S(1)} %copy-done.11, s32[4]{0:T(128)S(1)} %copy-done.15, f32[4,256,128]{2,1,0:T(8,128)S(1)} %copy-done.2, f32[4,256]{1,0:T(4,128)S(1)} %copy-done.16, f32[4,256]{1,0:T(4,128)S(1)} %tile.10.live_ref, f32[1,256,128]{2,1,0:T(8,128)S(1)} %copy-done.9, ...), custom_call_target="tpu_custom_call" | custom-call | tf_op jit(solution)/shard_map/pallas_call | solution.py:741
  (54 shorter events, 2.5 us)
Async XLA Ops:
  2.7 35.2 %copy-start.20 = (s32[4,32]{1,0:T(4,128)S(1)}, s32[4,32]{1,0:T(4,128)}, u32[]{:S(2)}) copy-start(s32[4,32]{1,0:T(4,128)} %param.11) | copy-start | bytes 1540
  2.7 24.8 %collective-permute-start.3 = (bf16[3,576,256]{2,1,0:T(8,128)(2,1)}, bf16[3,576,256]{2,1,0:T(8,128)(2,1)S(1)}, u32[]{:S(2)}, u32[]{:S(2)}) collective-permute-start(bf16[3,576,256]{2,1,0:T(8,128)(2,1)} %get-tuple-element.27.refs_0_), channel_id=1, source_target_pairs={{4,0},{8,4},{12,8},{5,1},{9,5},{13,9},{6,2},{10,6},{14,10},{7,3},{... | collective-permute-start | bytes 2654216 | tf_op jit(solution)/shard_map/ppermute | solution.py:832
  4.0 25.9 %collective-permute-start.2 = (bf16[3,576,256]{2,1,0:T(8,128)(2,1)}, bf16[3,576,256]{2,1,0:T(8,128)(2,1)S(1)}, u32[]{:S(2)}, u32[]{:S(2)}) collective-permute-start(bf16[3,576,256]{2,1,0:T(8,128)(2,1)} %get-tuple-element.27.refs_0_), channel_id=1, source_target_pairs={{0,4},{4,8},{8,12},{1,5},{5,9},{9,13},{2,6},{6,10},{10,14},{3,7},{... | collective-permute-start | bytes 2654216 | tf_op jit(solution)/shard_map/ppermute | solution.py:832
  9.7 42.4 %collective-permute-start.1 = (bf16[1,576,256]{2,1,0:T(8,128)(2,1)}, bf16[1,576,256]{2,1,0:T(8,128)(2,1)S(1)}, u32[]{:S(2)}, u32[]{:S(2)}) collective-permute-start(bf16[1,576,256]{2,1,0:T(8,128)(2,1)} %get-tuple-element.28.refs_1_.refs_3_), channel_id=1, source_target_pairs={{8,4},{12,8},{9,5},{13,9},{10,6},{14,10},{11,7},{15,11},{24,20},{2... | collective-permute-start | bytes 884744 | tf_op jit(solution)/shard_map/ppermute | solution.py:832
  10.4 41.8 %collective-permute-start = (bf16[1,576,256]{2,1,0:T(8,128)(2,1)}, bf16[1,576,256]{2,1,0:T(8,128)(2,1)S(1)}, u32[]{:S(2)}, u32[]{:S(2)}) collective-permute-start(bf16[1,576,256]{2,1,0:T(8,128)(2,1)} %get-tuple-element.28.refs_1_.refs_3_), channel_id=1, source_target_pairs={{0,4},{4,8},{1,5},{5,9},{2,6},{6,10},{3,7},{7,11},{16,20},{20,24},... | collective-permute-start | bytes 884744 | tf_op jit(solution)/shard_map/ppermute | solution.py:832
  27.6 21.6 %copy-start.23 = (bf16[3,576,256]{2,1,0:T(8,128)(2,1)}, bf16[3,576,256]{2,1,0:T(8,128)(2,1)S(1)}, u32[]{:S(2)}) copy-start(bf16[3,576,256]{2,1,0:T(8,128)(2,1)S(1)} %collective-permute-done.3.refs_1_) | copy-start | bytes 2654212
  30.0 20.5 %copy-start.22 = (bf16[3,576,256]{2,1,0:T(8,128)(2,1)}, bf16[3,576,256]{2,1,0:T(8,128)(2,1)S(1)}, u32[]{:S(2)}) copy-start(bf16[3,576,256]{2,1,0:T(8,128)(2,1)S(1)} %collective-permute-done.2.refs_0_) | copy-start | bytes 2654212
  32.7 28.0 %collective-permute-start.9 = (bf16[896,512]{1,0:T(8,128)(2,1)}, bf16[896,512]{1,0:T(8,128)(2,1)}, u32[]{:S(2)}, u32[]{:S(2)}) collective-permute-start(bf16[896,512]{1,0:T(8,128)(2,1)} %shard_map.95), channel_id=1, source_target_pairs={{0,4},{12,8},{1,5},{13,9},{2,6},{14,10},{3,7},{15,11},{16,20},{28,... | collective-permute-start | bytes 2752520 | tf_op jit(solution)/shard_map/ppermute | solution.py:832
  49.2 24.7 %collective-permute-start.8 = (bf16[3,576,256]{2,1,0:T(8,128)(2,1)S(1)}, bf16[3,576,256]{2,1,0:T(8,128)(2,1)}, u32[]{:S(2)}, u32[]{:S(2)}) collective-permute-start(bf16[3,576,256]{2,1,0:T(8,128)(2,1)S(1)} %collective-permute-done.3.refs_1_), channel_id=1, source_target_pairs={{4,0},{8,4},{5,1},{9,5},{6,2},{10,6},{7,3},{11,7},{20,16},{24,20},... | collective-permute-start | bytes 2654216 | tf_op jit(solution)/shard_map/ppermute | solution.py:832
  50.5 24.7 %collective-permute-start.5 = (bf16[3,576,256]{2,1,0:T(8,128)(2,1)S(1)}, bf16[3,576,256]{2,1,0:T(8,128)(2,1)}, u32[]{:S(2)}, u32[]{:S(2)}) collective-permute-start(bf16[3,576,256]{2,1,0:T(8,128)(2,1)S(1)} %collective-permute-done.2.refs_0_), channel_id=1, source_target_pairs={{4,8},{8,12},{5,9},{9,13},{6,10},{10,14},{7,11},{11,15},{20,24},{2... | collective-permute-start | bytes 2654216 | tf_op jit(solution)/shard_map/ppermute | solution.py:832
  52.1 23.8 %copy-start.18 = (bf16[1,576,256]{2,1,0:T(8,128)(2,1)}, bf16[1,576,256]{2,1,0:T(8,128)(2,1)S(1)}, u32[]{:S(2)}) copy-start(bf16[1,576,256]{2,1,0:T(8,128)(2,1)S(1)} %collective-permute-done.1.refs_1_) | copy-start | bytes 884740
  52.1 23.8 %copy-start.19 = (bf16[1,576,256]{2,1,0:T(8,128)(2,1)}, bf16[1,576,256]{2,1,0:T(8,128)(2,1)S(1)}, u32[]{:S(2)}) copy-start(bf16[1,576,256]{2,1,0:T(8,128)(2,1)S(1)} %collective-permute-done.refs_0_) | copy-start | bytes 884740
  60.7 30.6 %collective-permute-start.10 = (bf16[896,512]{1,0:T(8,128)(2,1)}, bf16[896,512]{1,0:T(8,128)(2,1)}, u32[]{:S(2)}, u32[]{:S(2)}) collective-permute-start(bf16[896,512]{1,0:T(8,128)(2,1)} %collective-permute-done.9.refs_4_), channel_id=1, source_target_pairs={{4,5},{5,4},{6,7},{7,6},{8,9},{9,8},{10,11},{11,10},{20,21},{21,20... | collective-permute-start | bytes 2752520 | tf_op jit(solution)/shard_map/ppermute | solution.py:853
  62.3 15.7 %collective-permute-start.6 = (bf16[3,272,128]{2,1,0:T(8,128)(2,1)}, bf16[3,272,128]{2,1,0:T(8,128)(2,1)S(1)}, u32[]{:S(2)}, u32[]{:S(2)}) collective-permute-start(bf16[3,272,128]{2,1,0:T(8,128)(2,1)} %get-tuple-element.32), channel_id=1, source_target_pairs={{4,0},{8,4},{12,8},{5,1},{9,5},{13,9},{6,2},{10,6},{14,10},{7,3},{... | collective-permute-start | bytes 626696 | tf_op jit(solution)/shard_map/ppermute | solution.py:832
  63.6 15.8 %collective-permute-start.7 = (bf16[3,272,128]{2,1,0:T(8,128)(2,1)}, bf16[3,272,128]{2,1,0:T(8,128)(2,1)S(1)}, u32[]{:S(2)}, u32[]{:S(2)}) collective-permute-start(bf16[3,272,128]{2,1,0:T(8,128)(2,1)} %get-tuple-element.33), channel_id=1, source_target_pairs={{0,4},{4,8},{8,12},{1,5},{5,9},{9,13},{2,6},{6,10},{10,14},{3,7},{... | collective-permute-start | bytes 626696 | tf_op jit(solution)/shard_map/ppermute | solution.py:832
  73.9 28.4 %collective-permute-start.13 = (bf16[3,576,256]{2,1,0:T(8,128)(2,1)}, bf16[3,576,256]{2,1,0:T(8,128)(2,1)S(1)}, u32[]{:S(2)}, u32[]{:S(2)}) collective-permute-start(bf16[3,576,256]{2,1,0:T(8,128)(2,1)} %collective-permute-done.8.refs_1_), channel_id=1, source_target_pairs={{4,0},{5,1},{6,2},{7,3},{20,16},{21,17},{22,18},{23,19}} | collective-permute-start | bytes 2654216 | tf_op jit(solution)/shard_map/ppermute | solution.py:832
  75.2 26.7 %collective-permute-start.12 = (bf16[3,576,256]{2,1,0:T(8,128)(2,1)}, bf16[3,576,256]{2,1,0:T(8,128)(2,1)S(1)}, u32[]{:S(2)}, u32[]{:S(2)}) collective-permute-start(bf16[3,576,256]{2,1,0:T(8,128)(2,1)} %collective-permute-done.5.refs_0_), channel_id=1, source_target_pairs={{8,12},{9,13},{10,14},{11,15},{24,28},{25,29},{26,30},{27,31}} | collective-permute-start | bytes 2654216 | tf_op jit(solution)/shard_map/ppermute | solution.py:832
  78.0 0.7 copy-start.3
  78.7 12.6 %collective-permute-start.4 = (bf16[1,576,256]{2,1,0:T(8,128)(2,1)}, bf16[1,576,256]{2,1,0:T(8,128)(2,1)S(1)}, u32[]{:S(2)}, u32[]{:S(2)}) collective-permute-start(bf16[1,576,256]{2,1,0:T(8,128)(2,1)} %broadcast_select_fusion), channel_id=1, source_target_pairs={{4,8},{8,4},{5,9},{9,5},{6,10},{10,6},{7,11},{11,7},{20,24},{24,20... | collective-permute-start | bytes 884744 | tf_op jit(solution)/shard_map/ppermute | solution.py:832
  79.4 0.7 copy-start.5
  88.4 13.9 %copy-start = (bf16[32,512,128]{2,1,0:T(8,128)(2,1)S(1)}, bf16[32,512,128]{2,1,0:T(8,128)(2,1)}, u32[]{:S(2)}) copy-start(bf16[32,512,128]{2,1,0:T(8,128)(2,1)} %refs_4_.7) | copy-start | bytes 12582916
  88.4 13.8 %copy-start.1 = (bf16[4,64,1536]{2,1,0:T(8,128)(2,1)S(1)}, bf16[4,64,1536]{2,1,0:T(8,128)(2,1)}, u32[]{:S(2)}) copy-start(bf16[4,64,1536]{2,1,0:T(8,128)(2,1)} %refs_3_.7) | copy-start | bytes 2359300
  88.4 12.8 %collective-permute-start.11 = (bf16[3,272,128]{2,1,0:T(8,128)(2,1)}, bf16[3,272,128]{2,1,0:T(8,128)(2,1)S(1)}, u32[]{:S(2)}, u32[]{:S(2)}) collective-permute-start(bf16[3,272,128]{2,1,0:T(8,128)(2,1)} %shard_map.94), channel_id=1, source_target_pairs={{8,0},{12,4},{0,8},{4,12},{9,1},{13,5},{1,9},{5,13},{10,2},{14,6},... | collective-permute-start | bytes 626696 | tf_op jit(solution)/shard_map/ppermute | solution.py:832
  91.3 0.7 copy-start.24
  101.2 0.7 copy-start.7
  101.9 23.8 %copy-start.2 = (f32[4,256,128]{2,1,0:T(8,128)S(1)}, f32[4,256,128]{2,1,0:T(8,128)}, u32[]{:S(2)}) copy-start(f32[4,256,128]{2,1,0:T(8,128)} %get-tuple-element.29.part_ref) | copy-start | bytes 1572868
  102.3 0.7 copy-start.10
  102.9 0.7 copy-start.12
  103.6 0.7 copy-start.14
  104.3 15.6 %copy-start.21 = (s32[4,32]{1,0:T(4,128)S(1)}, s32[4,32]{1,0:T(4,128)}, u32[]{:S(2)}) copy-start(s32[4,32]{1,0:T(4,128)} %param.12) | copy-start | bytes 1540
  112.5 13.3 %collective-permute-start.14 = (bf16[3,272,128]{2,1,0:T(8,128)(2,1)}, bf16[3,272,128]{2,1,0:T(8,128)(2,1)S(1)}, u32[]{:S(2)}, u32[]{:S(2)}) collective-permute-start(bf16[3,272,128]{2,1,0:T(8,128)(2,1)} %shard_map.97), channel_id=1, source_target_pairs={{0,12},{12,0},{1,13},{13,1},{2,14},{14,2},{3,15},{15,3},{16,28},{2... | collective-permute-start | bytes 626696 | tf_op jit(solution)/shard_map/ppermute | solution.py:832
  116.5 3.4 %collective-permute-start.16 = (bf16[1,272,128]{2,1,0:T(8,128)(2,1)}, bf16[1,272,128]{2,1,0:T(8,128)(2,1)S(1)}, u32[]{:S(2)}, u32[]{:S(2)}) collective-permute-start(bf16[1,272,128]{2,1,0:T(8,128)(2,1)} %get-tuple-element.47), channel_id=1, source_target_pairs={{4,8},{8,4},{5,9},{9,5},{6,10},{10,6},{7,11},{11,7},{20,24},{24,20... | collective-permute-start | bytes 208904 | tf_op jit(solution)/shard_map/ppermute | solution.py:832
  117.2 7.3 %collective-permute-start.17 = (bf16[1,272,128]{2,1,0:T(8,128)(2,1)}, bf16[1,272,128]{2,1,0:T(8,128)(2,1)S(1)}, u32[]{:S(2)}, u32[]{:S(2)}) collective-permute-start(bf16[1,272,128]{2,1,0:T(8,128)(2,1)} %get-tuple-element.48), channel_id=1, source_target_pairs={{8,0},{4,12},{9,1},{5,13},{10,2},{6,14},{11,3},{7,15},{24,16},{20,... | collective-permute-start | bytes 208904 | tf_op jit(solution)/shard_map/ppermute | solution.py:832
  118.5 7.2 %collective-permute-start.15 = (bf16[1,272,128]{2,1,0:T(8,128)(2,1)}, bf16[1,272,128]{2,1,0:T(8,128)(2,1)S(1)}, u32[]{:S(2)}, u32[]{:S(2)}) collective-permute-start(bf16[1,272,128]{2,1,0:T(8,128)(2,1)} %get-tuple-element.44), channel_id=1, source_target_pairs={{4,0},{8,12},{5,1},{9,13},{6,2},{10,14},{7,3},{11,15},{20,16},{24,... | collective-permute-start | bytes 208904 | tf_op jit(solution)/shard_map/ppermute | solution.py:832
  125.8 0.9 copy-start.4
  126.7 0.9 copy-start.6
  127.6 0.9 copy-start.8
  128.6 0.9 copy-start.9
  129.5 0.7 copy-start.11
  130.1 0.7 copy-start.13
  130.8 0.7 copy-start.15
  131.4 0.7 copy-start.16
  132.1 0.7 copy-start.17
where the time goes:
time: 136 us; the launch traced here: 135 us
  starting transfers between devices  46.3 us (34%)
  Pallas kernels  45.2 us (33%)
  waiting for transfers between devices  29.2 us (21%)
  local copies, waits for them, and re-layouts  12.5 us (9%)
  other arithmetic  1.48 us (1%)
    pallas_call x8, Pallas kernels, call(): pl.pallas_call(kernel, in_specs=[spec for spec, _ in operands], out_specs...  45.2 us
    ppermute x17, starting transfers between devices, shift(): return lax.ppermute(value, 'blk', pairs)  44.7 us
    ppermute x17, waiting for transfers between devices, shift(): return lax.ppermute(value, 'blk', pairs)  29.2 us
    unnamed x50, local copies, waits for them, and re-layouts  11.8 us
  transfers between devices with their start and end apart: 18, of which 7 were waited for; matrix products, arithmetic and copies ran while one was open for 2% of the time, Pallas kernels for 24%

commit v1 on v0

--- a/solution.py
+++ b/solution.py
@@ -794,10 +794,10 @@
     half = page_rows // 2
     pieces = rope_pieces(half, dim_lat)
 
-    def answer(steps, query_groups, own=(), space=HBM, limit=VMEM_LIMIT):
+    def answer(steps, query_groups, own=()):
         lanes = len(steps)
         count = request_count if own else most
-        operands = scalars + [(space, query) for group in query_groups for query in group]
+        operands = scalars + [(HBM, query) for group in query_groups for query in group]
         if own:
             operands += [(HBM, own[0])]
         operands += pages
@@ -825,7 +825,6 @@
                 dma((lanes,)),
             ],
             unit_flops * lanes * count,
-            limit,
         )
 
     def shift(value, pairs):
@@ -859,7 +858,7 @@
     apart_far = shift(after(crossing, *first), [(1, size - 2), (size - 2, 1)])
     right3 = shift(after(right2, *first), [(size - 2, size - 1)])
     left3 = shift(after(left2, *first), [(1, 0)])
-    (second,) = answer([[-2, 2]], [[after(right2, from_right, from_left), left2]])
+    (second,) = answer([[-2, 2]], [[right2, left2]])
     from_far = shift(second, [(i, i - 2) for i in range(2, size)] + [(i, i + 2) for i in range(size - 2)])
     outer, inner, distant, apart_part, apart_stat = call(
         functools.partial(hub_kernel, block, scale),
@@ -892,9 +891,7 @@
     from_hub = shift(outer, [(1, 0), (size - 2, size - 1)])
     from_other = shift(inner, [(1, size - 2), (size - 2, 1)])
     from_distant = shift(distant, [(size - 2, 0), (1, size - 1)])
-    (third,) = answer(
-        [[1 - size, size - 1]], [[after(right3, outer, from_far), left3]], space=VMEM, limit=44 << 20
-    )
+    (third,) = answer([[1 - size, size - 1]], [[after(right3, outer), left3]])
     from_end = shift(third, [(0, size - 1), (size - 1, 0)])
     layout = [[1], [-1], [-2, 2], [1 - size, size - 1], False, True, False]
     arrays = (

time: 136 us -> 122 us (0.90)
  local copies, waits for them, and re-layouts: 12.5 us -> 1.69 us
  starting transfers between devices: 46.3 us -> 37.9 us
  waiting for transfers between devices: 29.2 us -> 35.1 us
    unnamed x50 -> x42, local copies, waits for them, and re-layouts: 11.8 us -> 1.01 us
    ppermute x17, starting transfers between devices: 44.7 us -> 36.3 us  [shift(): return lax.ppermute(value, 'blk', pairs)]
    ppermute x17, waiting for transfers between devices: 29.2 us -> 35.1 us  [shift(): return lax.ppermute(value, 'blk', pairs)]
  transfers between devices with their start and end apart: 18 -> 18, of which waited for: 7 -> 6; matrix products, arithmetic and copies ran while one was open for 2% -> 1% of each run, Pallas kernels for 24% -> 33%
where the time goes in v1:
time: 122 us; the launch traced here: 121 us
  Pallas kernels  45.2 us (37%)
  starting transfers between devices  37.9 us (31%)
  waiting for transfers between devices  35.1 us (29%)
  local copies, waits for them, and re-layouts  1.69 us (1%)
    pallas_call x8, Pallas kernels, call(): pl.pallas_call(kernel, in_specs=[spec for spec, _ in operands], out_specs...  45.2 us
    ppermute x17, starting transfers between devices, shift(): return lax.ppermute(value, 'blk', pairs)  36.3 us
    ppermute x17, waiting for transfers between devices, shift(): return lax.ppermute(value, 'blk', pairs)  35.1 us
  transfers between devices with their start and end apart: 18, of which 6 were waited for; matrix products, arithmetic and copies ran while one was open for 1% of the time, Pallas kernels for 33%

profile of v1, /device:TPU:0, one launch (start us, length us, event | category | flops | bytes accessed | tf_op | source)
XLA Modules:
  0.0 121.1 jit_solution(4954759984485873860)
XLA Ops:
  0.0 2.7 %shard_map.91 = (bf16[3,576,256]{2,1,0:T(8,128)(2,1)}, bf16[1,576,256]{2,1,0:T(8,128)(2,1)}) custom-call(s32[4]{0:T(128)} %length_ref.14, bf16[4,576,256]{2,1,0:T(8,128)(2,1)} %query_ref.1), custom_call_target="tpu_custom_call" | custom-call | tf_op jit(solution)/shard_map/pallas_call | solution.py:741
  2.7 0.0 copy-start.13
  2.8 5.9 %collective-permute-start.2 = (bf16[3,576,256]{2,1,0:T(8,128)(2,1)}, bf16[3,576,256]{2,1,0:T(8,128)(2,1)}, u32[]{:S(2)}, u32[]{:S(2)}) collective-permute-start(bf16[3,576,256]{2,1,0:T(8,128)(2,1)} %get-tuple-element.26.refs_0_), channel_id=1, source_target_pairs={{0,4},{4,8},{8,12},{1,5},{5,9},{9,13},{2,6},{6,10},{10,14},{3,7},{... | collective-permute-start | bytes 2654216 | tf_op jit(solution)/shard_map/ppermute | solution.py:831
  8.7 1.3 %collective-permute-start.3 = (bf16[3,576,256]{2,1,0:T(8,128)(2,1)}, bf16[3,576,256]{2,1,0:T(8,128)(2,1)}, u32[]{:S(2)}, u32[]{:S(2)}) collective-permute-start(bf16[3,576,256]{2,1,0:T(8,128)(2,1)} %get-tuple-element.26.refs_0_), channel_id=1, source_target_pairs={{4,0},{8,4},{12,8},{5,1},{9,5},{13,9},{6,2},{10,6},{14,10},{7,3},{... | collective-permute-start | bytes 2654216 | tf_op jit(solution)/shard_map/ppermute | solution.py:831
  10.0 4.6 %collective-permute-start = (bf16[1,576,256]{2,1,0:T(8,128)(2,1)}, bf16[1,576,256]{2,1,0:T(8,128)(2,1)S(1)}, u32[]{:S(2)}, u32[]{:S(2)}) collective-permute-start(bf16[1,576,256]{2,1,0:T(8,128)(2,1)} %get-tuple-element.27.refs_1_.refs_3_), channel_id=1, source_target_pairs={{0,4},{4,8},{1,5},{5,9},{2,6},{6,10},{3,7},{7,11},{16,20},{20,24},... | collective-permute-start | bytes 884744 | tf_op jit(solution)/shard_map/ppermute | solution.py:831
  14.5 0.7 collective-permute-start.1
  15.2 0.6 pad_add_fusion.place_ref
  15.8 12.2 %collective-permute-done.2.refs_0_ = bf16[3,576,256]{2,1,0:T(8,128)(2,1)} collective-permute-done((bf16[3,576,256]{2,1,0:T(8,128)(2,1)}, bf16[3,576,256]{2,1,0:T(8,128)(2,1)}, u32[]{:S(2)}, u32[]{:S(2)}) %collective-permute-start.2) | collective-permute-done | bytes 884768 | tf_op jit(solution)/shard_map/ppermute | solution.py:831
  28.1 3.9 %collective-permute-done.3.refs_1_ = bf16[3,576,256]{2,1,0:T(8,128)(2,1)} collective-permute-done((bf16[3,576,256]{2,1,0:T(8,128)(2,1)}, bf16[3,576,256]{2,1,0:T(8,128)(2,1)}, u32[]{:S(2)}, u32[]{:S(2)}) %collective-permute-start.3) | collective-permute-done | bytes 884768 | tf_op jit(solution)/shard_map/ppermute | solution.py:831
  32.0 2.8 %shard_map.95 = bf16[896,512]{1,0:T(8,128)(2,1)} custom-call(s32[3]{0:T(128)} %pad_add_fusion.place_ref, s32[4]{0:T(128)} %length_ref.14, bf16[4,1536,512]{2,1,0:T(8,128)(2,1)} %refs_2_.7, bf16[4,64,1536]{2,1,0:T(8,128)(2,1)} %refs_3_.7), custom_call_target="tpu_custom_call" | custom-call | tf_op jit(solution)/shard_map/pallas_call | solution.py:741
  34.8 4.0 %collective-permute-start.7 = (bf16[896,512]{1,0:T(8,128)(2,1)}, bf16[896,512]{1,0:T(8,128)(2,1)S(1)}, u32[]{:S(2)}, u32[]{:S(2)}) collective-permute-start(bf16[896,512]{1,0:T(8,128)(2,1)} %shard_map.95), channel_id=1, source_target_pairs={{0,4},{12,8},{1,5},{13,9},{2,6},{14,10},{3,7},{15,11},{16,20},{28,... | collective-permute-start | bytes 2752520 | tf_op jit(solution)/shard_map/ppermute | solution.py:831
  38.8 0.1 broadcast_add_fusion
  38.9 0.6 reshape.12.refs_6_
  39.5 10.6 %shard_map.92 = (f32[4,256,128]{2,1,0:T(8,128)}, f32[4,256]{1,0:T(4,128)}) custom-call(s32[3]{0:T(128)} %pad_add_fusion.place_ref, s32[4]{0:T(128)} %length_ref.14, s32[4]{0:T(128)} %start_ref.11, bf16[3,576,256]{2,1,0:T(8,128)(2,1)} %get-tuple-element.26.refs_0_, bf16[1,576,256]{2,1,0:T(8,128)(2,1)} %get-tuple-element.27.refs_1_.refs_3_, ...), custom_call_target="tpu_custom_call" | custom-call | flops 3422552064 | bytes 13369344 | tf_op jit(solution)/shard_map/pallas_call | solution.py:741
  50.0 0.7 collective-permute-start.5
  50.8 1.3 %collective-permute-start.6 = (bf16[3,576,256]{2,1,0:T(8,128)(2,1)}, bf16[3,576,256]{2,1,0:T(8,128)(2,1)S(1)}, u32[]{:S(2)}, u32[]{:S(2)}) collective-permute-start(bf16[3,576,256]{2,1,0:T(8,128)(2,1)} %collective-permute-done.3.refs_1_), channel_id=1, source_target_pairs={{4,0},{8,4},{5,1},{9,5},{6,2},{10,6},{7,3},{11,7},{20,16},{24,20},... | collective-permute-start | bytes 2654216 | tf_op jit(solution)/shard_map/ppermute | solution.py:831
  52.1 0.0 collective-permute-done.refs_0_
  52.1 0.0 collective-permute-done.1.refs_1_
  52.1 8.6 %shard_map.93 = (bf16[3,272,128]{2,1,0:T(8,128)(2,1)}, bf16[3,272,128]{2,1,0:T(8,128)(2,1)}) custom-call(s32[3]{0:T(128)} %pad_add_fusion.place_ref, s32[4]{0:T(128)} %length_ref.14, s32[4]{0:T(128)} %start_ref.11, bf16[3,576,256]{2,1,0:T(8,128)(2,1)} %collective-permute-done.2.refs_0_, bf16[3,576,256]{2,1,0:T(8,128)(2,1)} %collective-permute-done.3.refs_1_, ...), custom_call_target="tpu_custom_call" | custom-call | flops 5133828096 | bytes 20054016 | tf_op jit(solution)/shard_map/pallas_call | solution.py:741
  60.7 0.0 collective-permute-done.7.refs_4_
  60.7 1.6 %collective-permute-start.8 = (bf16[896,512]{1,0:T(8,128)(2,1)S(1)}, bf16[896,512]{1,0:T(8,128)(2,1)}, u32[]{:S(2)}, u32[]{:S(2)}) collective-permute-start(bf16[896,512]{1,0:T(8,128)(2,1)S(1)} %collective-permute-done.7.refs_4_), channel_id=1, source_target_pairs={{4,5},{5,4},{6,7},{7,6},{8,9},{9,8},{10,11},{11,10},{20,21},{21,20... | collective-permute-start | bytes 2752520 | tf_op jit(solution)/shard_map/ppermute | solution.py:852
  62.3 0.0 collective-permute-done.5.refs_0_
  62.3 0.7 collective-permute-start.12
  63.0 8.4 %collective-permute-done.6.refs_1_ = bf16[3,576,256]{2,1,0:T(8,128)(2,1)S(1)} collective-permute-done((bf16[3,576,256]{2,1,0:T(8,128)(2,1)}, bf16[3,576,256]{2,1,0:T(8,128)(2,1)S(1)}, u32[]{:S(2)}, u32[]{:S(2)}) %collective-permute-start.6) | collective-permute-done | bytes 884768 | tf_op jit(solution)/shard_map/ppermute | solution.py:831
  71.4 1.3 %collective-permute-start.13 = (bf16[3,576,256]{2,1,0:T(8,128)(2,1)S(1)}, bf16[3,576,256]{2,1,0:T(8,128)(2,1)S(1)}, u32[]{:S(2)}, u32[]{:S(2)}) collective-permute-start(bf16[3,576,256]{2,1,0:T(8,128)(2,1)S(1)} %collective-permute-done.6.refs_1_), channel_id=1, source_target_pairs={{4,0},{5,1},{6,2},{7,3},{20,16},{21,17},{22,18},{23,19}} | collective-permute-start | bytes 2654216 | tf_op jit(solution)/shard_map/ppermute | solution.py:831
  72.8 0.8 collective-permute-start.4
  73.6 1.3 %collective-permute-start.9 = (bf16[3,272,128]{2,1,0:T(8,128)(2,1)}, bf16[3,272,128]{2,1,0:T(8,128)(2,1)S(1)}, u32[]{:S(2)}, u32[]{:S(2)}) collective-permute-start(bf16[3,272,128]{2,1,0:T(8,128)(2,1)} %get-tuple-element.31), channel_id=1, source_target_pairs={{4,0},{8,4},{12,8},{5,1},{9,5},{13,9},{6,2},{10,6},{14,10},{7,3},{... | collective-permute-start | bytes 626696 | tf_op jit(solution)/shard_map/ppermute | solution.py:831
  74.9 8.3 %shard_map.94 = bf16[3,272,128]{2,1,0:T(8,128)(2,1)} custom-call(s32[3]{0:T(128)} %pad_add_fusion.place_ref, s32[4]{0:T(128)} %length_ref.14, s32[4]{0:T(128)} %start_ref.11, bf16[3,576,256]{2,1,0:T(8,128)(2,1)} %copy-done.7, bf16[3,576,256]{2,1,0:T(8,128)(2,1)} %copy-done.8, bf16[4,1536,512]{2,1,0:T(8,128)(2,1)} %refs_2_.7, bf16[4,64,1536]{2,1,0:T(8,128)(2,1)} %refs_3_.7, ...), custom_call_target="tpu_custom_call" | custom-call | flops 2566914048 | bytes 10027008 | tf_op jit(solution)/shard_map/pallas_call | solution.py:741
  83.3 6.6 %collective-permute-start.10 = (bf16[3,272,128]{2,1,0:T(8,128)(2,1)S(1)}, bf16[3,272,128]{2,1,0:T(8,128)(2,1)S(1)}, u32[]{:S(2)}, u32[]{:S(2)}) collective-permute-start(bf16[3,272,128]{2,1,0:T(8,128)(2,1)S(1)} %copy-done.17), channel_id=1, source_target_pairs={{0,4},{4,8},{8,12},{1,5},{5,9},{9,13},{2,6},{6,10},{10,14},{3,7},{... | collective-permute-start | bytes 626696 | tf_op jit(solution)/shard_map/ppermute | solution.py:831
  89.9 0.0 collective-permute-done.8.refs_5_
  89.9 2.0 %collective-permute-start.11 = (bf16[3,272,128]{2,1,0:T(8,128)(2,1)}, bf16[3,272,128]{2,1,0:T(8,128)(2,1)S(1)}, u32[]{:S(2)}, u32[]{:S(2)}) collective-permute-start(bf16[3,272,128]{2,1,0:T(8,128)(2,1)} %shard_map.94), channel_id=1, source_target_pairs={{8,0},{12,4},{0,8},{4,12},{9,1},{13,5},{1,9},{5,13},{10,2},{14,6},... | collective-permute-start | bytes 626696 | tf_op jit(solution)/shard_map/ppermute | solution.py:831
  92.0 1.6 %shard_map.96 = (bf16[1,272,128]{2,1,0:T(8,128)(2,1)}, bf16[1,272,128]{2,1,0:T(8,128)(2,1)}, bf16[1,272,128]{2,1,0:T(8,128)(2,1)}, f32[1,256,128]{2,1,0:T(8,128)}, f32[1,256]{1,0:T(1,128)}) custom-call(s32[3]{0:T(128)} %pad_add_fusion.place_ref, s32[4]{0:T(128)} %length_ref.14, s32[4]{0:T(128)} %start_ref.11, bf16[1,576,256]{2,1,0:T(8,128)(2,1)} %copy-done.11, ...), custom_call_target="tpu_custom_call" | custom-call | flops 5989466112 | bytes 23396352 | tf_op jit(solution)/shard_map/pallas_call | solution.py:741
  93.6 0.0 collective-permute-done.12.refs_0_
  93.6 0.0 copy-start.14
  93.7 0.0 copy-start.2
  93.7 0.0 copy-start.4
  93.7 2.1 %collective-permute-done.13.refs_1_ = bf16[3,576,256]{2,1,0:T(8,128)(2,1)S(1)} collective-permute-done((bf16[3,576,256]{2,1,0:T(8,128)(2,1)S(1)}, bf16[3,576,256]{2,1,0:T(8,128)(2,1)S(1)}, u32[]{:S(2)}, u32[]{:S(2)}) %collective-permute-start.13) | collective-permute-done | bytes 884768 | tf_op jit(solution)/shard_map/ppermute | solution.py:831
  95.8 0.9 copy-done.10
  96.7 8.3 %shard_map.97 = bf16[3,272,128]{2,1,0:T(8,128)(2,1)} custom-call(s32[3]{0:T(128)} %pad_add_fusion.place_ref, s32[4]{0:T(128)} %length_ref.14, s32[4]{0:T(128)} %start_ref.11, bf16[3,576,256]{2,1,0:T(8,128)(2,1)} %copy-done.9, bf16[3,576,256]{2,1,0:T(8,128)(2,1)} %copy-done.10, bf16[4,1536,512]{2,1,0:T(8,128)(2,1)} %refs_2_.7, bf16[4,64,1536]{2,1,0:T(8,128)(2,1)} %refs_3_.7, ...), custom_call_target="tpu_custom_call" | custom-call | flops 2566914048 | bytes 10027008 | tf_op jit(solution)/shard_map/pallas_call | solution.py:741
  105.1 1.9 %collective-permute-start.14 = (bf16[3,272,128]{2,1,0:T(8,128)(2,1)}, bf16[3,272,128]{2,1,0:T(8,128)(2,1)S(1)}, u32[]{:S(2)}, u32[]{:S(2)}) collective-permute-start(bf16[3,272,128]{2,1,0:T(8,128)(2,1)} %shard_map.97), channel_id=1, source_target_pairs={{0,12},{12,0},{1,13},{13,1},{2,14},{14,2},{3,15},{15,3},{16,28},{2... | collective-permute-start | bytes 626696 | tf_op jit(solution)/shard_map/ppermute | solution.py:831
  107.0 1.3 %collective-permute-start.15 = (bf16[1,272,128]{2,1,0:T(8,128)(2,1)S(1)}, bf16[1,272,128]{2,1,0:T(8,128)(2,1)S(1)}, u32[]{:S(2)}, u32[]{:S(2)}) collective-permute-start(bf16[1,272,128]{2,1,0:T(8,128)(2,1)S(1)} %copy-done.20), channel_id=1, source_target_pairs={{4,0},{8,12},{5,1},{9,13},{6,2},{10,14},{7,3},{11,15},{20,16},{24,... | collective-permute-start | bytes 208904 | tf_op jit(solution)/shard_map/ppermute | solution.py:831
  108.3 0.0 collective-permute-done.9.refs_0_
  108.3 0.7 collective-permute-start.16
  109.0 1.3 %collective-permute-start.17 = (bf16[1,272,128]{2,1,0:T(8,128)(2,1)S(1)}, bf16[1,272,128]{2,1,0:T(8,128)(2,1)S(1)}, u32[]{:S(2)}, u32[]{:S(2)}) collective-permute-start(bf16[1,272,128]{2,1,0:T(8,128)(2,1)S(1)} %copy-done.18), channel_id=1, source_target_pairs={{8,0},{4,12},{9,1},{5,13},{10,2},{6,14},{11,3},{7,15},{24,16},{20,... | collective-permute-start | bytes 208904 | tf_op jit(solution)/shard_map/ppermute | solution.py:831
  110.4 0.1 tile.10.live_ref
  110.4 5.0 %collective-permute-done.15.refs_4_ = bf16[1,272,128]{2,1,0:T(8,128)(2,1)S(1)} collective-permute-done((bf16[1,272,128]{2,1,0:T(8,128)(2,1)S(1)}, bf16[1,272,128]{2,1,0:T(8,128)(2,1)S(1)}, u32[]{:S(2)}, u32[]{:S(2)}) %collective-permute-start.15) | collective-permute-done | bytes 69664 | tf_op jit(solution)/shard_map/ppermute | solution.py:831
  115.5 3.4 %collective-permute-done.17.refs_6_ = bf16[1,272,128]{2,1,0:T(8,128)(2,1)S(1)} collective-permute-done((bf16[1,272,128]{2,1,0:T(8,128)(2,1)S(1)}, bf16[1,272,128]{2,1,0:T(8,128)(2,1)S(1)}, u32[]{:S(2)}, u32[]{:S(2)}) %collective-permute-start.17) | collective-permute-done | bytes 69664 | tf_op jit(solution)/shard_map/ppermute | solution.py:831
  118.9 2.2 %shard_map.98 = bf16[4,32,1024]{2,1,0:T(8,128)(2,1)} custom-call(s32[3]{0:T(128)S(1)} %copy-done.3, s32[4]{0:T(128)S(1)} %copy-done.2, s32[4]{0:T(128)S(1)} %copy-done.4, f32[4,256,128]{2,1,0:T(8,128)S(1)} %copy-done, f32[4,256]{1,0:T(4,128)S(1)} %copy-done.5, f32[4,256]{1,0:T(4,128)S(1)} %tile.10.live_ref, f32[1,256,128]{2,1,0:T(8,128)S(1)} %copy-done.1, ...), custom_call_target="tpu_custom_call" | custom-call | tf_op jit(solution)/shard_map/pallas_call | solution.py:741
  (46 shorter events, 0.1 us)
Async XLA Ops:
  2.7 36.1 %copy-start.13 = (s32[4,32]{1,0:T(4,128)S(1)}, s32[4,32]{1,0:T(4,128)}, u32[]{:S(2)}) copy-start(s32[4,32]{1,0:T(4,128)} %param.11) | copy-start | bytes 1540
  2.8 25.3 %collective-permute-start.2 = (bf16[3,576,256]{2,1,0:T(8,128)(2,1)}, bf16[3,576,256]{2,1,0:T(8,128)(2,1)}, u32[]{:S(2)}, u32[]{:S(2)}) collective-permute-start(bf16[3,576,256]{2,1,0:T(8,128)(2,1)} %get-tuple-element.26.refs_0_), channel_id=1, source_target_pairs={{0,4},{4,8},{8,12},{1,5},{5,9},{9,13},{2,6},{6,10},{10,14},{3,7},{... | collective-permute-start | bytes 2654216 | tf_op jit(solution)/shard_map/ppermute | solution.py:831
  8.7 23.3 %collective-permute-start.3 = (bf16[3,576,256]{2,1,0:T(8,128)(2,1)}, bf16[3,576,256]{2,1,0:T(8,128)(2,1)}, u32[]{:S(2)}, u32[]{:S(2)}) collective-permute-start(bf16[3,576,256]{2,1,0:T(8,128)(2,1)} %get-tuple-element.26.refs_0_), channel_id=1, source_target_pairs={{4,0},{8,4},{12,8},{5,1},{9,5},{13,9},{6,2},{10,6},{14,10},{7,3},{... | collective-permute-start | bytes 2654216 | tf_op jit(solution)/shard_map/ppermute | solution.py:831
  10.0 42.1 %collective-permute-start = (bf16[1,576,256]{2,1,0:T(8,128)(2,1)}, bf16[1,576,256]{2,1,0:T(8,128)(2,1)S(1)}, u32[]{:S(2)}, u32[]{:S(2)}) collective-permute-start(bf16[1,576,256]{2,1,0:T(8,128)(2,1)} %get-tuple-element.27.refs_1_.refs_3_), channel_id=1, source_target_pairs={{0,4},{4,8},{1,5},{5,9},{2,6},{6,10},{3,7},{7,11},{16,20},{20,24},... | collective-permute-start | bytes 884744 | tf_op jit(solution)/shard_map/ppermute | solution.py:831
  14.5 37.6 %collective-permute-start.1 = (bf16[1,576,256]{2,1,0:T(8,128)(2,1)}, bf16[1,576,256]{2,1,0:T(8,128)(2,1)S(1)}, u32[]{:S(2)}, u32[]{:S(2)}) collective-permute-start(bf16[1,576,256]{2,1,0:T(8,128)(2,1)} %get-tuple-element.27.refs_1_.refs_3_), channel_id=1, source_target_pairs={{8,4},{12,8},{9,5},{13,9},{10,6},{14,10},{11,7},{15,11},{24,20},{2... | collective-permute-start | bytes 884744 | tf_op jit(solution)/shard_map/ppermute | solution.py:831
  34.8 25.9 %collective-permute-start.7 = (bf16[896,512]{1,0:T(8,128)(2,1)}, bf16[896,512]{1,0:T(8,128)(2,1)S(1)}, u32[]{:S(2)}, u32[]{:S(2)}) collective-permute-start(bf16[896,512]{1,0:T(8,128)(2,1)} %shard_map.95), channel_id=1, source_target_pairs={{0,4},{12,8},{1,5},{13,9},{2,6},{14,10},{3,7},{15,11},{16,20},{28,... | collective-permute-start | bytes 2752520 | tf_op jit(solution)/shard_map/ppermute | solution.py:831
  50.0 12.2 %collective-permute-start.5 = (bf16[3,576,256]{2,1,0:T(8,128)(2,1)}, bf16[3,576,256]{2,1,0:T(8,128)(2,1)S(1)}, u32[]{:S(2)}, u32[]{:S(2)}) collective-permute-start(bf16[3,576,256]{2,1,0:T(8,128)(2,1)} %collective-permute-done.2.refs_0_), channel_id=1, source_target_pairs={{4,8},{8,12},{5,9},{9,13},{6,10},{10,14},{7,11},{11,15},{20,24},{2... | collective-permute-start | bytes 2654216 | tf_op jit(solution)/shard_map/ppermute | solution.py:831
  50.8 20.7 %collective-permute-start.6 = (bf16[3,576,256]{2,1,0:T(8,128)(2,1)}, bf16[3,576,256]{2,1,0:T(8,128)(2,1)S(1)}, u32[]{:S(2)}, u32[]{:S(2)}) collective-permute-start(bf16[3,576,256]{2,1,0:T(8,128)(2,1)} %collective-permute-done.3.refs_1_), channel_id=1, source_target_pairs={{4,0},{8,4},{5,1},{9,5},{6,2},{10,6},{7,3},{11,7},{20,16},{24,20},... | collective-permute-start | bytes 2654216 | tf_op jit(solution)/shard_map/ppermute | solution.py:831
  52.1 20.6 %copy-start.11 = (bf16[1,576,256]{2,1,0:T(8,128)(2,1)}, bf16[1,576,256]{2,1,0:T(8,128)(2,1)S(1)}, u32[]{:S(2)}) copy-start(bf16[1,576,256]{2,1,0:T(8,128)(2,1)S(1)} %collective-permute-done.refs_0_) | copy-start | bytes 884740
  52.1 20.6 %copy-start.12 = (bf16[1,576,256]{2,1,0:T(8,128)(2,1)}, bf16[1,576,256]{2,1,0:T(8,128)(2,1)S(1)}, u32[]{:S(2)}) copy-start(bf16[1,576,256]{2,1,0:T(8,128)(2,1)S(1)} %collective-permute-done.1.refs_1_) | copy-start | bytes 884740
  60.7 31.3 %copy-start.15 = (bf16[896,512]{1,0:T(8,128)(2,1)}, bf16[896,512]{1,0:T(8,128)(2,1)S(1)}, u32[]{:S(2)}) copy-start(bf16[896,512]{1,0:T(8,128)(2,1)S(1)} %collective-permute-done.7.refs_4_) | copy-start | bytes 2752516
  60.7 29.2 %collective-permute-start.8 = (bf16[896,512]{1,0:T(8,128)(2,1)S(1)}, bf16[896,512]{1,0:T(8,128)(2,1)}, u32[]{:S(2)}, u32[]{:S(2)}) collective-permute-start(bf16[896,512]{1,0:T(8,128)(2,1)S(1)} %collective-permute-done.7.refs_4_), channel_id=1, source_target_pairs={{4,5},{5,4},{6,7},{7,6},{8,9},{9,8},{10,11},{11,10},{20,21},{21,20... | collective-permute-start | bytes 2752520 | tf_op jit(solution)/shard_map/ppermute | solution.py:852
  62.3 12.6 %copy-start.7 = (bf16[3,576,256]{2,1,0:T(8,128)(2,1)}, bf16[3,576,256]{2,1,0:T(8,128)(2,1)S(1)}, u32[]{:S(2)}) copy-start(bf16[3,576,256]{2,1,0:T(8,128)(2,1)S(1)} %collective-permute-done.5.refs_0_) | copy-start | bytes 2654212
  62.3 31.3 %collective-permute-start.12 = (bf16[3,576,256]{2,1,0:T(8,128)(2,1)S(1)}, bf16[3,576,256]{2,1,0:T(8,128)(2,1)S(1)}, u32[]{:S(2)}, u32[]{:S(2)}) collective-permute-start(bf16[3,576,256]{2,1,0:T(8,128)(2,1)S(1)} %collective-permute-done.5.refs_0_), channel_id=1, source_target_pairs={{8,12},{9,13},{10,14},{11,15},{24,28},{25,29},{26,30},{27,31}} | collective-permute-start | bytes 2654216 | tf_op jit(solution)/shard_map/ppermute | solution.py:831
  71.4 3.5 %copy-start.8 = (bf16[3,576,256]{2,1,0:T(8,128)(2,1)}, bf16[3,576,256]{2,1,0:T(8,128)(2,1)S(1)}, u32[]{:S(2)}) copy-start(bf16[3,576,256]{2,1,0:T(8,128)(2,1)S(1)} %collective-permute-done.6.refs_1_) | copy-start | bytes 2654212
  71.4 24.4 %collective-permute-start.13 = (bf16[3,576,256]{2,1,0:T(8,128)(2,1)S(1)}, bf16[3,576,256]{2,1,0:T(8,128)(2,1)S(1)}, u32[]{:S(2)}, u32[]{:S(2)}) collective-permute-start(bf16[3,576,256]{2,1,0:T(8,128)(2,1)S(1)} %collective-permute-done.6.refs_1_), channel_id=1, source_target_pairs={{4,0},{5,1},{6,2},{7,3},{20,16},{21,17},{22,18},{23,19}} | collective-permute-start | bytes 2654216 | tf_op jit(solution)/shard_map/ppermute | solution.py:831
  72.8 10.5 %copy-start.17 = (bf16[3,272,128]{2,1,0:T(8,128)(2,1)S(1)}, bf16[3,272,128]{2,1,0:T(8,128)(2,1)}, u32[]{:S(2)}) copy-start(bf16[3,272,128]{2,1,0:T(8,128)(2,1)} %get-tuple-element.32) | copy-start | bytes 626692
  72.8 10.5 %collective-permute-start.4 = (bf16[1,576,256]{2,1,0:T(8,128)(2,1)S(1)}, bf16[1,576,256]{2,1,0:T(8,128)(2,1)S(1)}, u32[]{:S(2)}, u32[]{:S(2)}) collective-permute-start(bf16[1,576,256]{2,1,0:T(8,128)(2,1)S(1)} %broadcast_select_fusion), channel_id=1, source_target_pairs={{4,8},{8,4},{5,9},{9,5},{6,10},{10,6},{7,11},{11,7},{20,24},{24,20... | collective-permute-start | bytes 884744 | tf_op jit(solution)/shard_map/ppermute | solution.py:831
  73.6 34.7 %collective-permute-start.9 = (bf16[3,272,128]{2,1,0:T(8,128)(2,1)}, bf16[3,272,128]{2,1,0:T(8,128)(2,1)S(1)}, u32[]{:S(2)}, u32[]{:S(2)}) collective-permute-start(bf16[3,272,128]{2,1,0:T(8,128)(2,1)} %get-tuple-element.31), channel_id=1, source_target_pairs={{4,0},{8,4},{12,8},{5,1},{9,5},{13,9},{6,2},{10,6},{14,10},{7,3},{... | collective-permute-start | bytes 626696 | tf_op jit(solution)/shard_map/ppermute | solution.py:831
  83.3 8.7 %copy-start.16 = (bf16[1,576,256]{2,1,0:T(8,128)(2,1)}, bf16[1,576,256]{2,1,0:T(8,128)(2,1)S(1)}, u32[]{:S(2)}) copy-start(bf16[1,576,256]{2,1,0:T(8,128)(2,1)S(1)} %collective-permute-done.4.refs_2_) | copy-start | bytes 884740
  83.3 25.7 %collective-permute-start.10 = (bf16[3,272,128]{2,1,0:T(8,128)(2,1)S(1)}, bf16[3,272,128]{2,1,0:T(8,128)(2,1)S(1)}, u32[]{:S(2)}, u32[]{:S(2)}) collective-permute-start(bf16[3,272,128]{2,1,0:T(8,128)(2,1)S(1)} %copy-done.17), channel_id=1, source_target_pairs={{0,4},{4,8},{8,12},{1,5},{5,9},{9,13},{2,6},{6,10},{10,14},{3,7},{... | collective-permute-start | bytes 626696 | tf_op jit(solution)/shard_map/ppermute | solution.py:831
  89.9 20.5 %collective-permute-start.11 = (bf16[3,272,128]{2,1,0:T(8,128)(2,1)}, bf16[3,272,128]{2,1,0:T(8,128)(2,1)S(1)}, u32[]{:S(2)}, u32[]{:S(2)}) collective-permute-start(bf16[3,272,128]{2,1,0:T(8,128)(2,1)} %shard_map.94), channel_id=1, source_target_pairs={{8,0},{12,4},{0,8},{4,12},{9,1},{13,5},{1,9},{5,13},{10,2},{14,6},... | collective-permute-start | bytes 626696 | tf_op jit(solution)/shard_map/ppermute | solution.py:831
  93.6 2.2 %copy-start.9 = (bf16[3,576,256]{2,1,0:T(8,128)(2,1)}, bf16[3,576,256]{2,1,0:T(8,128)(2,1)S(1)}, u32[]{:S(2)}) copy-start(bf16[3,576,256]{2,1,0:T(8,128)(2,1)S(1)} %collective-permute-done.12.refs_0_) | copy-start | bytes 2654212
  93.6 13.4 %copy-start.20 = (bf16[1,272,128]{2,1,0:T(8,128)(2,1)S(1)}, bf16[1,272,128]{2,1,0:T(8,128)(2,1)}, u32[]{:S(2)}) copy-start(bf16[1,272,128]{2,1,0:T(8,128)(2,1)} %get-tuple-element.42) | copy-start | bytes 208900
  93.6 14.7 %copy-start.19 = (bf16[1,272,128]{2,1,0:T(8,128)(2,1)S(1)}, bf16[1,272,128]{2,1,0:T(8,128)(2,1)}, u32[]{:S(2)}) copy-start(bf16[1,272,128]{2,1,0:T(8,128)(2,1)} %get-tuple-element.45) | copy-start | bytes 208900
  93.6 15.4 %copy-start.18 = (bf16[1,272,128]{2,1,0:T(8,128)(2,1)S(1)}, bf16[1,272,128]{2,1,0:T(8,128)(2,1)}, u32[]{:S(2)}) copy-start(bf16[1,272,128]{2,1,0:T(8,128)(2,1)} %get-tuple-element.46) | copy-start | bytes 208900
  93.6 16.7 %copy-start.14 = (s32[4,32]{1,0:T(4,128)S(1)}, s32[4,32]{1,0:T(4,128)}, u32[]{:S(2)}) copy-start(s32[4,32]{1,0:T(4,128)} %param.12) | copy-start | bytes 1540
  93.6 25.2 %copy-start = (f32[4,256,128]{2,1,0:T(8,128)S(1)}, f32[4,256,128]{2,1,0:T(8,128)}, u32[]{:S(2)}) copy-start(f32[4,256,128]{2,1,0:T(8,128)} %get-tuple-element.28.part_ref) | copy-start | bytes 1572868
  93.6 25.2 %copy-start.1 = (f32[1,256,128]{2,1,0:T(8,128)S(1)}, f32[1,256,128]{2,1,0:T(8,128)}, u32[]{:S(2)}) copy-start(f32[1,256,128]{2,1,0:T(8,128)} %get-tuple-element.39.apart_ref) | copy-start | bytes 393220
  93.7 25.2 %copy-start.2 = (s32[4]{0:T(128)S(1)}, s32[4]{0:T(128)}, u32[]{:S(2)}) copy-start(s32[4]{0:T(128)} %length_ref.14) | copy-start | bytes 52
  93.7 25.2 %copy-start.3 = (s32[3]{0:T(128)S(1)}, s32[3]{0:T(128)}, u32[]{:S(2)}) copy-start(s32[3]{0:T(128)} %pad_add_fusion.place_ref) | copy-start | bytes 40
  93.7 25.2 %copy-start.4 = (s32[4]{0:T(128)S(1)}, s32[4]{0:T(128)}, u32[]{:S(2)}) copy-start(s32[4]{0:T(128)} %start_ref.11) | copy-start | bytes 52
  93.7 25.2 %copy-start.5 = (f32[4,256]{1,0:T(4,128)S(1)}, f32[4,256]{1,0:T(4,128)}, u32[]{:S(2)}) copy-start(f32[4,256]{1,0:T(4,128)} %get-tuple-element.29.stat_ref) | copy-start | bytes 12292
  93.7 25.2 %copy-start.6 = (f32[1,256]{1,0:T(1,128)S(1)}, f32[1,256]{1,0:T(1,128)}, u32[]{:S(2)}) copy-start(f32[1,256]{1,0:T(1,128)} %get-tuple-element.40.apart_stat_ref) | copy-start | bytes 3076
  95.8 0.9 copy-start.10
  105.1 13.8 %collective-permute-start.14 = (bf16[3,272,128]{2,1,0:T(8,128)(2,1)}, bf16[3,272,128]{2,1,0:T(8,128)(2,1)S(1)}, u32[]{:S(2)}, u32[]{:S(2)}) collective-permute-start(bf16[3,272,128]{2,1,0:T(8,128)(2,1)} %shard_map.97), channel_id=1, source_target_pairs={{0,12},{12,0},{1,13},{13,1},{2,14},{14,2},{3,15},{15,3},{16,28},{2... | collective-permute-start | bytes 626696 | tf_op jit(solution)/shard_map/ppermute | solution.py:831
  107.0 8.4 %collective-permute-start.15 = (bf16[1,272,128]{2,1,0:T(8,128)(2,1)S(1)}, bf16[1,272,128]{2,1,0:T(8,128)(2,1)S(1)}, u32[]{:S(2)}, u32[]{:S(2)}) collective-permute-start(bf16[1,272,128]{2,1,0:T(8,128)(2,1)S(1)} %copy-done.20), channel_id=1, source_target_pairs={{4,0},{8,12},{5,1},{9,13},{6,2},{10,14},{7,3},{11,15},{20,16},{24,... | collective-permute-start | bytes 208904 | tf_op jit(solution)/shard_map/ppermute | solution.py:831
  108.3 7.1 %collective-permute-start.16 = (bf16[1,272,128]{2,1,0:T(8,128)(2,1)S(1)}, bf16[1,272,128]{2,1,0:T(8,128)(2,1)S(1)}, u32[]{:S(2)}, u32[]{:S(2)}) collective-permute-start(bf16[1,272,128]{2,1,0:T(8,128)(2,1)S(1)} %copy-done.19), channel_id=1, source_target_pairs={{4,8},{8,4},{5,9},{9,5},{6,10},{10,6},{7,11},{11,7},{20,24},{24,20... | collective-permute-start | bytes 208904 | tf_op jit(solution)/shard_map/ppermute | solution.py:831
  109.0 9.8 %collective-permute-start.17 = (bf16[1,272,128]{2,1,0:T(8,128)(2,1)S(1)}, bf16[1,272,128]{2,1,0:T(8,128)(2,1)S(1)}, u32[]{:S(2)}, u32[]{:S(2)}) collective-permute-start(bf16[1,272,128]{2,1,0:T(8,128)(2,1)S(1)} %copy-done.18), channel_id=1, source_target_pairs={{8,0},{4,12},{9,1},{5,13},{10,2},{6,14},{11,3},{7,15},{24,16},{20,... | collective-permute-start | bytes 208904 | tf_op jit(solution)/shard_map/ppermute | solution.py:831
